TPU v7x, 32 devices: a whole 2x2x4 slice. The times are simulated.
32 devices in a mesh: line: 1, freq: 4 (over z), section: 2 (over core), rcv: 4 (over y, x).
Axes of the slice: x: 2, y: 2, z: 4, core: 2. Of those that a mesh axis runs over, the one named last changes fastest.
Arguments:
- recorded: bfloat16 [512, 512, 1024], P(('line', 'freq', 'section'), 'rcv'), may hold values from -6 to 6
- signatures: bfloat16 [512, 256], P(('line', 'freq', 'section')), may hold values from -0.375 to 0.375
- ghost_delay: int32 [512, 512], P(('line', 'freq', 'section'), 'rcv'), may hold values from 8 to 47
- dead_trace: int32 [512, 512], P(('line', 'freq', 'section'), 'rcv'), may hold values 0 or 1
Outputs:
- multiples: float32 [2, 32, 512, 512], P(None, ('freq', 'section'), 'line', 'rcv')
All inputs are finite; a program needn't handle non-finite values. No bound on the sum of `dead_trace` on one device may be relied on, other than what follows from the above.
Results may differ from a plain program's by a relative error of at most 0.0041.
Values may be sent and summed in bfloat16 or wider, within the bound.
No kernel may reach another device: no remote copies, remote signals or barrier semaphores. Data moves between devices by JAX's collectives and lax.ppermute only.
A program may use at most 320 MiB of HBM per device.

v0:
```python
import math

import jax
import jax.numpy as jnp
from jax import lax
from jax.sharding import PartitionSpec as P

BIN_DEV = 1


reflectivity = 0.6


def filter_kernel(signatures):
    shot_count, tap_count = signatures.shape
    zero_front = jnp.zeros((shot_count, tap_count), signatures.dtype)
    zero_back = jnp.zeros((shot_count, tap_count + 1), signatures.dtype)
    padded = jnp.concatenate([zero_front, signatures, zero_back], axis=1)
    width = 3 * tap_count
    rows_count = 2 * tap_count
    tiled = jnp.tile(padded, (1, rows_count))[:, : rows_count * width]
    banded = tiled.reshape(shot_count, rows_count, width)
    return banded[:, :, 2 * tap_count :]


def designature(recorded, signatures):
    shot_count, receivers, samples = recorded.shape
    tap_count = signatures.shape[1]
    blocks = samples // tap_count
    kernel = filter_kernel(signatures)
    blocked = recorded.reshape(shot_count, receivers, blocks, tap_count)
    previous_partial = jnp.concatenate(
        [jnp.zeros_like(blocked[:, :, :1]), blocked[:, :, :-1]], axis=2
    )
    window = jnp.concatenate([previous_partial, blocked], axis=3)
    filtered = jnp.einsum("srbj,sji->srbi", window, kernel, preferred_element_type=jnp.float32)
    return filtered.reshape(shot_count, receivers, samples)


def spectrum(filtered, bin_count):
    samples = filtered.shape[2]
    sample_index = jnp.arange(samples, dtype=jnp.int32)
    bin_index = jnp.arange(1, bin_count + 1, dtype=jnp.int32)
    phase_angles = (bin_index[:, None] * sample_index[None, :] % samples).astype(jnp.float32) * (
        2.0 * math.pi / samples
    )
    factor = 1.0 / math.sqrt(samples)
    twiddle = jnp.stack([jnp.cos(phase_angles) * factor, -jnp.sin(phase_angles) * factor])
    return jnp.einsum("srt,pft->pfsr", filtered, twiddle, precision=lax.Precision.HIGHEST)


def deghost(spectra, ghost_delay, dead_trace, samples):
    bin_count = spectra.shape[1]
    bin_index = jnp.arange(1, bin_count + 1, dtype=jnp.int32)
    phase_angles = (bin_index[:, None, None] * ghost_delay[None] % samples).astype(jnp.float32) * (
        2.0 * math.pi / samples
    )
    cosine = jnp.cos(phase_angles)
    sine_value = jnp.sin(phase_angles)
    divisor = 1.0 - 2.0 * reflectivity * cosine + reflectivity * reflectivity
    gain_real = (1.0 - reflectivity * cosine) / divisor
    gain_imag = -reflectivity * sine_value / divisor
    live_mask = (1 - dead_trace).astype(jnp.float32)[None]
    real_part = (spectra[0] * gain_real - spectra[1] * gain_imag) * live_mask
    imag_part = (spectra[0] * gain_imag + spectra[1] * gain_real) * live_mask
    return jnp.stack([real_part, imag_part]).astype(jnp.bfloat16)


def multiply(left_operand, right_operand):
    return jnp.einsum(
        "uxy,uym->uxm", left_operand, right_operand, preferred_element_type=jnp.float32
    )


def complex_product(left_operand, right_operand):
    real_out = multiply(left_operand[0], right_operand[0]) - multiply(
        left_operand[1], right_operand[1]
    )
    imag_out = multiply(left_operand[0], right_operand[1]) + multiply(
        left_operand[1], right_operand[0]
    )
    return jnp.stack([real_out, imag_out])


def per_device(recorded, signatures, ghost_delay, dead_trace):
    samples = recorded.shape[2]
    bin_count = BIN_DEV * lax.axis_size("freq") * lax.axis_size("section") * lax.axis_size("rcv")
    filtered = designature(recorded, signatures)
    spectra = spectrum(filtered, bin_count)
    deghosted = deghost(spectra, ghost_delay, dead_trace, samples)
    relayed = lax.all_to_all(
        deghosted, ("freq", "section"), split_axis=1, concat_axis=2, tiled=True
    )
    summed = complex_product(lax.all_gather(relayed, "rcv", axis=3, tiled=True), relayed)
    station_count = relayed.shape[2]
    return summed * (1.0 / math.sqrt(station_count))


def solution(mesh):
    return jax.shard_map(
        per_device,
        mesh=mesh,
        in_specs=(
            P(("line", "freq", "section"), "rcv", None),
            P(("line", "freq", "section"), None),
            P(("line", "freq", "section"), "rcv"),
            P(("line", "freq", "section"), "rcv"),
        ),
        out_specs=P(None, ("freq", "section"), "line", "rcv"),
        check_vma=False,
    )
```

profile of v0, /device:TPU:0, one launch (start us, length us, event | category | flops | bytes accessed | tf_op | source)
XLA Modules:
  0.0 433.4 jit_solution(421783146112873044)
XLA Ops:
  6.5 0.0 all-gather.2.cloned.1.call-start
  6.5 22.3 %copy.16 = bf16[64,128,1024]{1,2,0:T(8,128)(2,1)} copy(bf16[64,128,1024]{2,1,0:T(8,128)(2,1)} %param.4) | data formatting | bytes 33554432 | tf_op args[0]
  28.8 22.4 %copy.17 = bf16[64,128,4,256]{3,1,2,0:T(8,128)(2,1)} copy(bf16[64,128,4,256]{1,3,2,0:T(8,128)(2,1)} %bitcast.49) | data formatting | bytes 33554432 | tf_op jit(solution)/shard_map/reshape | solution.py:31
  51.2 0.0 copy-start.1
  51.2 10.7 %slice.44 = bf16[64,128,3,256]{3,1,2,0:T(8,128)(2,1)} slice(bf16[64,128,4,256]{3,1,2,0:T(8,128)(2,1)} %copy.17), slice={[0:64], [0:128], [0:3], [0:256]} | slice | bytes 25165824 | tf_op jit(solution)/shard_map/slice | solution.py:33
  62.0 0.0 copy-done.1
  62.0 18.8 %tile.4 = bf16[64,512,769]{2,1,0:T(8,128)(2,1)} broadcast(bf16[64,769]{1,0:T(8,128)(2,1)S(1)} %maximum_maximum_fusion), dimensions={0,2} | broadcast | bytes 50495616 | tf_op jit(solution)/shard_map/tile | solution.py:21
  80.9 122.3 %tile.10 = bf16[64,393728]{1,0:T(8,128)(2,1)} reshape(bf16[64,512,769]{2,1,0:T(8,128)(2,1)} %tile.4) | data formatting | bytes 100794368 | tf_op jit(solution)/shard_map/tile | solution.py:21
  203.2 33.3 %slice.45 = bf16[64,393216]{1,0:T(8,128)(2,1)} slice(bf16[64,393728]{1,0:T(8,128)(2,1)} %tile.10), slice={[0:64], [0:393216]} | slice | bytes 100663296 | tf_op jit(solution)/shard_map/slice | solution.py:21
  236.5 0.0 copy-start.2
  236.5 34.2 %copy.28 = bf16[8,8,512,768]{3,2,1,0:T(8,128)(2,1)} copy(bf16[8,8,512,768]{3,1,2,0:T(8,128)(2,1)} %bitcast.48) | data formatting | bytes 100663296
  270.7 0.6 cosine_multiply_fusion
  271.3 0.0 copy-done.2
  271.3 29.4 %fusion.2 = f32[64,128,4,256]{1,3,2,0:T(8,128)} fusion(bf16[64,128,3,256]{3,1,2,0:T(8,128)(2,1)} %slice.44, bf16[64,128,4,256]{3,1,2,0:T(8,128)(2,1)} %copy.17, bf16[64,512,768]{2,1,0:T(8,128)(2,1)} %bitcast.50), kind=kOutput, calls=%fused_computation.3 | convolution fusion | flops 8690597888 | bytes 79691776 | tf_op jit(solution)/shard_map/srbj,sji->srbi/dot_general | solution.py:36
  300.7 0.0 copy-start
  300.7 24.1 %fusion.20 = f32[2,32,64,128]{3,1,2,0:T(8,128)S(1)} fusion(f32[64,128,1024,1]{1,2,0,3:T(8,128)} %bitcast.51, f32[1,32,1024]{2,1,0:T(8,128)S(1)} %get-tuple-element.12, f32[1,32,1024]{2,1,0:T(8,128)S(1)} %get-tuple-element.11), kind=kOutput, calls=%fused_computation.36 | convolution fusion | flops 6442516480 | bytes 35913728 | tf_op jit(solution)/shard_map/srt,pft->pfsr/dot_general | solution.py:49
  324.8 0.0 copy-done
  324.8 5.1 %multiply_convert_fusion.1 = (bf16[1,32,64,128]{3,1,2,0:T(8,128)(2,1)S(1)}, bf16[1,32,64,128]{3,1,2,0:T(8,128)(2,1)S(1)}) fusion(f32[2,32,64,128]{3,1,2,0:T(8,128)S(1)} %fusion.20, f32[64,128]{1,0:T(8,128)S(1)} %subtract_convert_fusion, s32[64,128]{1,0:T(8,128)S(1)} %copy-done, s32[32]{0:T(128)S(1)} %iota_add_fusion), kind=kLoop, calls=%fused_computation.30 | loop fusion | flops 8126464 | bytes 3211392 | tf_op jit(solution)/shard_map/convert
  329.9 0.1 pad_maximum_fusion
  330.0 0.4 copy.21
  330.4 32.7 %all_to_all.18 = bf16[2,32,64,128]{3,2,0,1:T(8,128)(2,1)S(1)} all-to-all(bf16[2,32,64,128]{3,2,0,1:T(8,128)(2,1)S(1)} %copy.21), channel_id=1, replica_groups=mesh['line'=1,'freq'=4,'section'=2,'rcv'=4] {'freq','section'}, dimensions={1} | all-to-all | bytes 2097152 | tf_op jit(solution)/shard_map/all_to_all | solution.py:91
  363.1 1.1 copy.31
  364.2 0.0 all-gather.2.cloned.1.call-update
  364.2 1.3 fusion.33
  365.5 50.3 %all-gather.2.cloned.1.call-done = bf16[2,4,512,512]{3,2,1,0:T(8,128)(2,1)} async-done(((bf16[2,4,512,128]{3,2,1,0:T(8,128)(2,1)}), bf16[2,4,512,512]{3,2,1,0:T(8,128)(2,1)}) %all-gather.2.cloned.1.call-update) | async-done | bytes 4194320 | tf_op jit(solution)/shard_map/all_gather | solution.py:94
  415.8 2.3 fusion.9
  418.1 2.3 fusion.8
  420.4 2.3 fusion.13
  422.8 2.3 fusion.15
  425.1 1.5 maximum_multiply_fusion
  (7 shorter events, 0.1 us)
Async XLA Ops:
  6.5 409.3 %all-gather.2.cloned.1.call-start = ((), (), s32[]{:S(2)}) async-start(), calls=%async_computation.1 | async-start | bytes 5242880 | tf_op jit(solution)/shard_map/all_gather | solution.py:94
  51.2 10.8 %copy-start.1 = (bf16[64,256]{1,0:T(8,128)(2,1)S(1)}, bf16[64,256]{1,0:T(8,128)(2,1)}, u32[]{:S(2)}) copy-start(bf16[64,256]{1,0:T(8,128)(2,1)} %param.5) | copy-start | bytes 98308
  236.5 34.8 %copy-start.2 = (s32[64,128]{1,0:T(8,128)S(1)}, s32[64,128]{1,0:T(8,128)}, u32[]{:S(2)}) copy-start(s32[64,128]{1,0:T(8,128)} %param.7) | copy-start | bytes 98308
  300.7 24.1 %copy-start = (s32[64,128]{1,0:T(8,128)S(1)}, s32[64,128]{1,0:T(8,128)}, u32[]{:S(2)}) copy-start(s32[64,128]{1,0:T(8,128)} %param.6) | copy-start | bytes 98308
Sparse Core Ops, SparseCore 0:
  364.3 51.4 all-gather.1
where the time goes:
time: 435 us; the launch traced here: 433 us
  local copies, waits for them, and re-layouts  267 us (61%)
  matrix products  62.7 us (14%)
  waiting for transfers between devices  50.3 us (12%)
  blocking collectives  32.7 us (8%)
  between operations  13.5 us (3%)
  other arithmetic  7.29 us (2%)
    another operation x2, local copies, waits for them, and re-layouts, filter_kernel(): tiled = jnp.tile(padded, (1, rows_count))[:, :rows_count * width]  141 us
    unnamed x8, local copies, waits for them, and re-layouts  56.5 us
    all_gather x1, waiting for transfers between devices, per_device(): lax.all_gather(relayed, 'rcv', axis=3, tiled=True)  50.3 us
    slice x1, local copies, waits for them, and re-layouts, filter_kernel(): tiled = jnp.tile(padded, (1, rows_count))[:, :rows_count * width]  33.3 us
    all_to_all x1, blocking collectives, per_device(): lax.all_to_all(deghosted, ('freq', 'section'), split_axis=1, concat_axis=...  32.7 us
    dot_general x1, matrix products, designature(): jnp.einsum('srbj,sji->srbi', window, kernel, preferred_element_type=jnp.f...  29.4 us
    dot_general x1, matrix products, spectrum(): jnp.einsum('srt,pft->pfsr', filtered, twiddle, precision=lax.Precision.HI...  24.1 us
    reshape x1, local copies, waits for them, and re-layouts, designature(): blocked = recorded.reshape(shot_count, receivers, blocks, tap_count)  22.4 us
  transfers between devices with their start and end apart: 1, of which 1 were waited for; matrix products, arithmetic and copies ran while one was open for 0% of the time, Pallas kernels for 0%

commit v1 on v0

v1 whole, which is shorter than its diff:
```python
import functools
import math

import jax
import jax.numpy as jnp
import ml_dtypes
import numpy as np
from jax import lax
from jax.experimental import pallas as pl
from jax.experimental.pallas import tpu as pltpu
from jax.sharding import PartitionSpec as P

REFLECTIVITY = 0.6
LANES = 128
BLOCK = 16
SPECTRUM_VMEM = 60 * 2**20
REGROUP_VMEM = 16 * 2**20
PRODUCT_VMEM = 24 * 2**20
COLLECT_VMEM = 16 * 2**20


def split_pair(values):
    high = values.astype(ml_dtypes.bfloat16)
    low = (values - high.astype(np.float64)).astype(ml_dtypes.bfloat16)
    return high, low


@functools.lru_cache(maxsize=None)
def tables(samples, taps, bins):
    bin_index = np.arange(1, bins + 1)[:, None]
    unit = 2.0 * math.pi / samples
    time_angle = (bin_index * np.arange(samples)[None] % samples) * unit
    head = samples - taps
    factor = 1.0 / math.sqrt(samples)
    twiddle = np.concatenate([np.cos(time_angle), -np.sin(time_angle)])
    head_high, head_low = split_pair(twiddle[:, :head])
    head_table = np.concatenate([head_high, head_low])
    tap_table = (twiddle[:, :taps] * factor).astype(np.float32)
    turn_table = twiddle[:, head:].astype(np.float32)
    lane = np.arange(taps)
    prefix = (lane[:, None] <= taps - 1 - lane[None]).astype(ml_dtypes.bfloat16)
    delay_angle = (bin_index * np.arange(LANES)[None] % samples) * unit
    gain = 1.0 / (1.0 - REFLECTIVITY * np.exp(-1j * delay_angle))
    gain[:, LANES - 1] = 0.0
    gain_table = np.concatenate([gain.real, gain.imag]).astype(np.float32)
    return head_table, tap_table, turn_table, prefix, gain_table


def halves(value):
    high = value.astype(jnp.bfloat16)
    low = (value - high.astype(jnp.float32)).astype(jnp.bfloat16)
    return jnp.concatenate([high, low])


def nt_dot(left, right):
    return lax.dot_general(
        left, right, (((1,), (1,)), ((), ())), preferred_element_type=jnp.float32
    )


def spectrum_body(place, bins, head_ref, tap_ref, turn_ref, prefix_ref, gain_ref, sig_ref, delay_ref, dead_ref, rec_ref, *rest):
    out_refs, rows_ref = rest[:-1], rest[-1]
    shots, receivers, samples = rec_ref.shape
    head = head_ref.shape[1]
    both = 2 * bins
    pulses = sig_ref[...].astype(jnp.float32)
    tap_table = tap_ref[...]
    parts = [halves(tap_table * pulses[shot : shot + 1]) for shot in range(shots)]
    sums = jnp.dot(
        jnp.concatenate(parts), prefix_ref[...], preferred_element_type=jnp.float32
    )
    turn_real, turn_imag = turn_ref[:bins], turn_ref[bins:]
    traces = rec_ref[...].reshape(shots * receivers, samples)
    whole = nt_dot(head_ref[...], traces[:, :head])
    whole = whole[:both] + whole[both:]
    lookup = jnp.where(dead_ref[...] != 0, LANES - 1, delay_ref[...])
    gain_table = gain_ref[...]
    for shot in range(shots):
        base = shot * 2 * both
        filt = sums[base : base + both] + sums[base + both : base + 2 * both]
        filt_real, filt_imag = filt[:bins], filt[bins:]
        tail_filter = jnp.concatenate(
            [
                filt_real * turn_real - filt_imag * turn_imag,
                filt_real * turn_imag + filt_imag * turn_real,
            ]
        )
        columns = slice(shot * receivers, (shot + 1) * receivers)
        tail = nt_dot(halves(tail_filter), traces[columns, head:])
        tail = tail[:both] + tail[both:]
        main_real, main_imag = whole[:bins, columns], whole[bins:, columns]
        pulse_real, pulse_imag = filt_real[:, :1], filt_imag[:, :1]
        real = main_real * pulse_real - main_imag * pulse_imag + tail[:bins]
        imag = main_real * pulse_imag + main_imag * pulse_real + tail[bins:]
        index = jnp.broadcast_to(lookup[shot : shot + 1], (both, receivers))
        gain = jnp.take_along_axis(gain_table, index, axis=1)
        gain_real, gain_imag = gain[:bins], gain[bins:]
        rows_ref[:bins, shot] = real * gain_real - imag * gain_imag
        rows_ref[bins:, shot] = real * gain_imag + imag * gain_real
    place(rows_ref, out_refs)


def spectrum_call(recorded, signatures, ghost_delay, dead_trace, bins, place, out_shapes, out_specs, first, count, block):
    samples, taps, receivers = recorded.shape[2], signatures.shape[1], recorded.shape[1]
    constants = [jnp.asarray(t) for t in tables(samples, taps, bins)]
    fixed = [pl.BlockSpec(t.shape, lambda i: (0, 0), pipeline_mode=pl.Buffered(1)) for t in constants]
    start = first // block
    rows = lambda width: pl.BlockSpec((block, width), lambda i: (i + start, 0))
    return pl.pallas_call(
        functools.partial(spectrum_body, place, bins),
        grid=(count // block,),
        in_specs=fixed
        + [rows(taps), rows(receivers), rows(receivers), pl.BlockSpec((block, receivers, samples), lambda i: (i + start, 0, 0))],
        out_specs=out_specs,
        out_shape=out_shapes,
        scratch_shapes=[pltpu.VMEM((2 * bins, block, receivers), jnp.float32)],
        compiler_params=pltpu.CompilerParams(vmem_limit_bytes=SPECTRUM_VMEM),
        cost_estimate=pl.CostEstimate(flops=2 * 2 * count * receivers * samples * 4 * bins // 2, bytes_accessed=count * receivers * samples * 2, transcendentals=0),
    )(*constants, signatures, ghost_delay, dead_trace, recorded)


def split_shots(shots):
    return [(0, shots, True)]


def axis_sizes():
    return lax.axis_size("freq"), lax.axis_size("section"), lax.axis_size("rcv")


def frequency_of(deep, side, across):
    sections, groups = lax.axis_size("section"), lax.axis_size("rcv")
    return (
        (lax.axis_index("freq") ^ deep) * sections + (lax.axis_index("section") ^ side)
    ) * groups + (lax.axis_index("rcv") ^ across)


def plane_offsets():
    _, sections, groups = axis_sizes()
    return [(side, across) for side in range(sections) for across in range(groups)]


def place_plain(rows_ref, out_refs):
    (out_ref,) = out_refs
    bins = out_ref.shape[0]
    for part in range(2):
        out_ref[:, part] = rows_ref[part * bins : (part + 1) * bins].astype(out_ref.dtype)


def place_relative(plane_first, rows_ref, out_refs):
    bins = rows_ref.shape[0] // 2
    for deep in range(lax.axis_size("freq")):
        for spot, (side, across) in enumerate(plane_offsets()):
            frequency = frequency_of(deep, side, across)
            outer, inner = (spot, deep) if plane_first else (deep, spot)
            for part in range(2):
                out_refs[outer][inner, part] = rows_ref[frequency + part * bins].astype(jnp.bfloat16)


def exchange(array, offset):
    if not any(offset):
        return array
    depths, sections, groups = axis_sizes()
    deep, side, across = offset
    pairs = [
        (
            (z * sections + s) * groups + c,
            ((z ^ deep) * sections + (s ^ side)) * groups + (c ^ across),
        )
        for z in range(depths)
        for s in range(sections)
        for c in range(groups)
    ]
    return lax.ppermute(array, ("freq", "section", "rcv"), pairs)


def exchange_plane(arrays):
    return [exchange(a, (0,) + o) for a, o in zip(arrays, plane_offsets(), strict=True)]


def exchange_deep(arrays):
    return [exchange(a, (deep, 0, 0)) for deep, a in enumerate(arrays)]


def regroup_body(count, *refs):
    in_refs, out_refs = refs[:count], refs[count:]
    for outer, out_ref in enumerate(out_refs):
        for inner in range(count):
            out_ref[inner] = in_refs[inner][outer]


def in_vmem(count):
    return [pl.BlockSpec(memory_space=pltpu.VMEM)] * count


def regroup(arrays):
    count, rest = arrays[0].shape[0], arrays[0].shape[1:]
    return pl.pallas_call(
        functools.partial(regroup_body, len(arrays)),
        out_shape=[jax.ShapeDtypeStruct((len(arrays),) + rest, jnp.bfloat16)] * count,
        in_specs=in_vmem(len(arrays)),
        out_specs=in_vmem(count),
        compiler_params=pltpu.CompilerParams(vmem_limit_bytes=REGROUP_VMEM),
        cost_estimate=pl.CostEstimate(flops=0, bytes_accessed=4 * len(arrays) * arrays[0].size, transcendentals=0),
    )(*arrays)


def spectra(recorded, signatures, ghost_delay, dead_trace, first, count, plane_first):
    depths, sections, groups = axis_sizes()
    plane = sections * groups
    receivers = recorded.shape[1]
    outer, inner = (plane, depths) if plane_first else (depths, plane)
    block = min(count, BLOCK)
    return spectrum_call(
        recorded,
        signatures,
        ghost_delay,
        dead_trace,
        plane * depths,
        functools.partial(place_relative, plane_first),
        [jax.ShapeDtypeStruct((inner, 2, count, receivers), jnp.bfloat16)] * outer,
        [pl.BlockSpec((inner, 2, block, receivers), lambda i: (0, 0, i, 0))] * outer,
        first,
        count,
        block,
    )


def product_body(pieces, *refs):
    sections, groups = lax.axis_size("section"), lax.axis_size("rcv")
    left_ref = refs[-1]
    out_refs = refs[-1 - groups : -1]
    in_refs = iter(refs)
    stations = left_ref.shape[0]
    receivers = stations // groups
    my_deep, my_side, my_across = (lax.axis_index(a) for a in ("freq", "section", "rcv"))
    offsets = plane_offsets()
    shots = stations // (lax.axis_size("freq") * sections)
    for plane_last, first, count in pieces:
        outer = lax.axis_size("freq") if not plane_last else len(offsets)
        for i in range(outer):
            ref = next(in_refs)
            for j in range(ref.shape[0]):
                deep, spot = (j, i) if plane_last else (i, j)
                side, across = offsets[spot]
                row = ((my_deep ^ deep) * sections + (my_side ^ side)) * shots + first
                row = pl.multiple_of(row, math.gcd(shots, first) if first else shots)
                column = (my_across ^ across) * receivers
                for part in range(2):
                    where = pl.multiple_of(column + part * stations, receivers)
                    left_ref[pl.ds(row, count), pl.ds(where, receivers)] = ref[j, part]
    left = left_ref[...]
    scale = 1.0 / math.sqrt(stations)
    for across in range(groups):
        column = pl.multiple_of((my_across ^ across) * receivers, receivers)
        real = left_ref[:, pl.ds(column, receivers)]
        imag = left_ref[:, pl.ds(pl.multiple_of(column + stations, receivers), receivers)]
        right = jnp.concatenate(
            [jnp.concatenate([real, imag], axis=1), jnp.concatenate([-imag, real], axis=1)]
        )
        both = jnp.dot(left, right, preferred_element_type=jnp.float32) * scale
        out_ref = out_refs[across]
        out_ref[0] = both[:, :receivers].astype(out_ref.dtype)
        out_ref[1] = both[:, receivers:].astype(out_ref.dtype)


def product(arrays, pieces, stations):
    groups = lax.axis_size("rcv")
    receivers = stations // groups
    return pl.pallas_call(
        functools.partial(product_body, pieces),
        out_shape=[
            jax.ShapeDtypeStruct((2, stations, receivers), jnp.bfloat16 if across else jnp.float32)
            for across in range(groups)
        ],
        in_specs=in_vmem(len(arrays)),
        out_specs=in_vmem(groups),
        scratch_shapes=[pltpu.VMEM((stations, 2 * stations), jnp.bfloat16)],
        compiler_params=pltpu.CompilerParams(vmem_limit_bytes=PRODUCT_VMEM),
        cost_estimate=pl.CostEstimate(flops=8 * stations**3, bytes_accessed=8 * stations**2, transcendentals=0),
    )(*arrays)


def collect_body(*refs):
    in_refs, out_ref = refs[:-1], refs[-1]
    mine = lax.axis_index("rcv")
    for across, ref in enumerate(in_refs):
        for part in range(2):
            out_ref[part, mine ^ across] = ref[part].astype(out_ref.dtype)


def collect(arrays):
    parts, stations, receivers = arrays[0].shape
    return pl.pallas_call(
        collect_body,
        out_shape=jax.ShapeDtypeStruct((parts, len(arrays), stations, receivers), jnp.float32),
        in_specs=in_vmem(len(arrays)),
        out_specs=pl.BlockSpec(memory_space=pltpu.VMEM),
        compiler_params=pltpu.CompilerParams(vmem_limit_bytes=COLLECT_VMEM),
    )(*arrays)


def few_devices(recorded, signatures, ghost_delay, dead_trace):
    stations = recorded.shape[1] * lax.axis_size("rcv")
    arrays, pieces = [], []
    for first, count, plane_first in split_shots(recorded.shape[0]):
        sent = spectra(recorded, signatures, ghost_delay, dead_trace, first, count, plane_first)
        steps = (exchange_plane, exchange_deep) if plane_first else (exchange_deep, exchange_plane)
        arrays += steps[1](regroup(steps[0](sent)))
        pieces.append((not plane_first, first, count))
    blocks = product(arrays, pieces, stations)
    return collect([exchange(b, (0, 0, across)) for across, b in enumerate(blocks)])


def many_devices(recorded, signatures, ghost_delay, dead_trace):
    shots, receivers, _ = recorded.shape
    depths, sections, groups = axis_sizes()
    bins = depths * sections * groups
    block = min(shots, BLOCK)
    (deghosted,) = spectrum_call(
        recorded,
        signatures,
        ghost_delay,
        dead_trace,
        bins,
        place_plain,
        [jax.ShapeDtypeStruct((bins, 2, shots, receivers), jnp.bfloat16)],
        [pl.BlockSpec((bins, 2, block, receivers), lambda i: (0, 0, i, 0))],
        0,
        shots,
        block,
    )
    axes = ("freq", "section", "rcv")
    relayed = lax.all_to_all(deghosted, axes, split_axis=0, concat_axis=0, tiled=True)
    relayed = relayed.reshape(depths * sections, groups, 2, shots, receivers)
    stations = groups * receivers
    matrix = jnp.transpose(relayed, (2, 0, 3, 1, 4)).reshape(2, stations, stations)
    real, imag = matrix[0], matrix[1]
    dot = functools.partial(jnp.dot, preferred_element_type=jnp.float32)
    whole = jnp.stack([dot(real, real) - dot(imag, imag), dot(real, imag) + dot(imag, real)])
    whole = (whole * (1.0 / math.sqrt(stations))).astype(jnp.bfloat16)
    whole = whole.reshape(2, stations, groups, receivers)
    whole = lax.all_to_all(whole, "rcv", split_axis=2, concat_axis=0, tiled=True)
    whole = whole.reshape(groups, 2, stations, receivers)
    return jnp.transpose(whole, (1, 0, 2, 3)).astype(jnp.float32)


def per_device(recorded, signatures, ghost_delay, dead_trace):
    sizes = axis_sizes()
    small = all(n & (n - 1) == 0 for n in sizes) and sizes[0] * sizes[1] * sizes[2] <= 32
    run = few_devices if small else many_devices
    return run(recorded, signatures, ghost_delay, dead_trace)


def solution(mesh):
    return jax.shard_map(
        per_device,
        mesh=mesh,
        in_specs=(
            P(("line", "freq", "section"), "rcv", None),
            P(("line", "freq", "section"), None),
            P(("line", "freq", "section"), "rcv"),
            P(("line", "freq", "section"), "rcv"),
        ),
        out_specs=P(None, ("freq", "section"), "line", "rcv"),
        check_vma=False,
    )
```

time: 435 us -> 71.4 us (0.16)
  the two profiles are of different devices: /device:TPU:0 before, /device:TPU:16 now
where the time goes in v1:
time: 71.4 us; the launch traced here: 71.2 us
  waiting for transfers between devices  42.7 us (60%)
  Pallas kernels  14 us (20%)
  starting transfers between devices  13.6 us (19%)
  local copies, waits for them, and re-layouts  0.91 us (1%)
    ppermute x13, waiting for transfers between devices, exchange(): return lax.ppermute(array, ('freq', 'section', 'rcv'), pairs)  42.7 us
    ppermute x13, starting transfers between devices, exchange(): return lax.ppermute(array, ('freq', 'section', 'rcv'), pairs)  13.6 us
    pallas_call x1, Pallas kernels, spectrum_call(): pl.pallas_call(functools.partial(spectrum_body, place, bins), grid=(count...  10.9 us
    pallas_call x1, Pallas kernels, product(): pl.pallas_call(functools.partial(product_body, pieces), out_shape=[jax.Sh...  1.56 us
    pallas_call x1, Pallas kernels, collect(): pl.pallas_call(collect_body, out_shape=jax.ShapeDtypeStruct((parts, len(a...  1.46 us
  transfers between devices with their start and end apart: 13, of which 9 were waited for; matrix products, arithmetic and copies ran while one was open for 0% of the time, Pallas kernels for 0%

profile of v1, /device:TPU:16, one launch (start us, length us, event | category | flops | bytes accessed | tf_op | source)
XLA Modules:
  0.0 71.2 jit_solution(17802354239076422915)
XLA Ops:
  0.0 10.9 %shard_map.91 = (bf16[4,2,64,128]{3,2,1,0:T(8,128)(2,1)}, bf16[4,2,64,128]{3,2,1,0:T(8,128)(2,1)}, bf16[4,2,64,128]{3,2,1,0:T(8,128)(2,1)}, bf16[4,2,64,128]{3,2...) custom-call(bf16[128,768]{1,0:T(8,128)(2,1)} %constant.10.clone.head, ...), custom_call_target="tpu_custom_call" | custom-call | flops 2147483648 | bytes 16777216 | tf_op jit(solution)/shard_map/pallas_call | solution.py:109
  10.9 1.6 %collective-permute-start = (bf16[4,2,64,128]{3,2,1,0:T(8,128)(2,1)}, bf16[4,2,64,128]{3,2,1,0:T(8,128)(2,1)S(1)}, u32[]{:S(2)}, u32[]{:S(2)}) collective-permute-start(bf16[4,2,64,128]{3,2,1,0:T(8,128)(2,1)} %get-tuple-element.22), channel_id=1, source_target_pairs={{0,1},{1,0},{2,3},{3,2},{4,5},{5,4},{6,7},{7,6},{8,9},{9,8},{10,11... | collective-permute-start | bytes 393224 | tf_op jit(solution)/shard_map/ppermute | solution.py:173
  12.4 1.5 %collective-permute-start.1 = (bf16[4,2,64,128]{3,2,1,0:T(8,128)(2,1)}, bf16[4,2,64,128]{3,2,1,0:T(8,128)(2,1)S(1)}, u32[]{:S(2)}, u32[]{:S(2)}) collective-permute-start(bf16[4,2,64,128]{3,2,1,0:T(8,128)(2,1)} %get-tuple-element.23), channel_id=1, source_target_pairs={{0,2},{1,3},{2,0},{3,1},{4,6},{5,7},{6,4},{7,5},{8,10},{9,11},{10,... | collective-permute-start | bytes 393224 | tf_op jit(solution)/shard_map/ppermute | solution.py:173
  13.9 0.5 collective-permute-start.2
  14.4 0.0 collective-permute-start.3
  14.4 1.6 %collective-permute-start.4 = (bf16[4,2,64,128]{3,2,1,0:T(8,128)(2,1)}, bf16[4,2,64,128]{3,2,1,0:T(8,128)(2,1)S(1)}, u32[]{:S(2)}, u32[]{:S(2)}) collective-permute-start(bf16[4,2,64,128]{3,2,1,0:T(8,128)(2,1)} %get-tuple-element.26), channel_id=1, source_target_pairs={{0,5},{1,4},{2,7},{3,6},{4,1},{5,0},{6,3},{7,2},{8,13},{9,12},{10,... | collective-permute-start | bytes 393224 | tf_op jit(solution)/shard_map/ppermute | solution.py:173
  16.0 0.7 %collective-permute-done.refs_1_ = bf16[4,2,64,128]{3,2,1,0:T(8,128)(2,1)S(1)} collective-permute-done((bf16[4,2,64,128]{3,2,1,0:T(8,128)(2,1)}, bf16[4,2,64,128]{3,2,1,0:T(8,128)(2,1)S(1)}, u32[]{:S(2)}, u32[]{:S(2)}) %collective-permute-start) | collective-permute-done | bytes 131104 | tf_op jit(solution)/shard_map/ppermute | solution.py:173
  16.8 0.4 collective-permute-start.5
  17.2 2.1 %collective-permute-done.1.refs_2_ = bf16[4,2,64,128]{3,2,1,0:T(8,128)(2,1)S(1)} collective-permute-done((bf16[4,2,64,128]{3,2,1,0:T(8,128)(2,1)}, bf16[4,2,64,128]{3,2,1,0:T(8,128)(2,1)S(1)}, u32[]{:S(2)}, u32[]{:S(2)}) %collective-permute-start.1) | collective-permute-done | bytes 131104 | tf_op jit(solution)/shard_map/ppermute | solution.py:173
  19.3 0.9 %collective-permute-start.6 = (bf16[4,2,64,128]{3,2,1,0:T(8,128)(2,1)}, bf16[4,2,64,128]{3,2,1,0:T(8,128)(2,1)S(1)}, u32[]{:S(2)}, u32[]{:S(2)}) collective-permute-start(bf16[4,2,64,128]{3,2,1,0:T(8,128)(2,1)} %get-tuple-element.28), channel_id=1, source_target_pairs={{0,7},{1,6},{2,5},{3,4},{4,3},{5,2},{6,1},{7,0},{8,15},{9,14},{10,... | collective-permute-start | bytes 393224 | tf_op jit(solution)/shard_map/ppermute | solution.py:173
  20.2 1.3 %collective-permute-done.2.refs_3_ = bf16[4,2,64,128]{3,2,1,0:T(8,128)(2,1)S(1)} collective-permute-done((bf16[4,2,64,128]{3,2,1,0:T(8,128)(2,1)}, bf16[4,2,64,128]{3,2,1,0:T(8,128)(2,1)S(1)}, u32[]{:S(2)}, u32[]{:S(2)}) %collective-permute-start.2) | collective-permute-done | bytes 131104 | tf_op jit(solution)/shard_map/ppermute | solution.py:173
  21.5 0.0 collective-permute-done.3.refs_4_
  21.5 0.0 collective-permute-done.4.refs_5_
  21.5 4.8 %collective-permute-done.5.refs_6_ = bf16[4,2,64,128]{3,2,1,0:T(8,128)(2,1)S(1)} collective-permute-done((bf16[4,2,64,128]{3,2,1,0:T(8,128)(2,1)}, bf16[4,2,64,128]{3,2,1,0:T(8,128)(2,1)S(1)}, u32[]{:S(2)}, u32[]{:S(2)}) %collective-permute-start.5) | collective-permute-done | bytes 131104 | tf_op jit(solution)/shard_map/ppermute | solution.py:173
  26.3 0.0 collective-permute-done.6.refs_7_
  26.3 0.0 copy-start
  26.3 0.9 %copy-done = bf16[4,2,64,128]{3,2,1,0:T(8,128)(2,1)S(1)} copy-done((bf16[4,2,64,128]{3,2,1,0:T(8,128)(2,1)S(1)}, bf16[4,2,64,128]{3,2,1,0:T(8,128)(2,1)}, u32[]{:S(2)}) %copy-start) | copy-done | bytes 131096
  27.2 0.1 shard_map.92
  27.3 1.6 %collective-permute-start.7 = (bf16[8,2,64,128]{3,2,1,0:T(8,128)(2,1)S(1)}, bf16[8,2,64,128]{3,2,1,0:T(8,128)(2,1)S(1)}, u32[]{:S(2)}, u32[]{:S(2)}) collective-permute-start(bf16[8,2,64,128]{3,2,1,0:T(8,128)(2,1)S(1)} %get-tuple-element.30), channel_id=1, source_target_pairs={{0,8},{1,9},{2,10},{3,11},{4,12},{5,13},{6,14},{7,15},{8,0},{9,1},... | collective-permute-start | bytes 786440 | tf_op jit(solution)/shard_map/ppermute | solution.py:173
  29.0 0.3 collective-permute-start.8
  29.3 1.6 %collective-permute-start.9 = (bf16[8,2,64,128]{3,2,1,0:T(8,128)(2,1)S(1)}, bf16[8,2,64,128]{3,2,1,0:T(8,128)(2,1)S(1)}, u32[]{:S(2)}, u32[]{:S(2)}) collective-permute-start(bf16[8,2,64,128]{3,2,1,0:T(8,128)(2,1)S(1)} %get-tuple-element.32), channel_id=1, source_target_pairs={{0,24},{1,25},{2,26},{3,27},{4,28},{5,29},{6,30},{7,31},{8,16},{9,... | collective-permute-start | bytes 786440 | tf_op jit(solution)/shard_map/ppermute | solution.py:173
  30.9 8.3 %collective-permute-done.7.refs_1_ = bf16[8,2,64,128]{3,2,1,0:T(8,128)(2,1)S(1)} collective-permute-done((bf16[8,2,64,128]{3,2,1,0:T(8,128)(2,1)S(1)}, bf16[8,2,64,128]{3,2,1,0:T(8,128)(2,1)S(1)}, u32[]{:S(2)}, u32[]{:S(2)}) %collective-permute-start.7) | collective-permute-done | bytes 262176 | tf_op jit(solution)/shard_map/ppermute | solution.py:173
  39.2 8.1 %collective-permute-done.8.refs_2_ = bf16[8,2,64,128]{3,2,1,0:T(8,128)(2,1)S(1)} collective-permute-done((bf16[8,2,64,128]{3,2,1,0:T(8,128)(2,1)S(1)}, bf16[8,2,64,128]{3,2,1,0:T(8,128)(2,1)S(1)}, u32[]{:S(2)}, u32[]{:S(2)}) %collective-permute-start.8) | collective-permute-done | bytes 262176 | tf_op jit(solution)/shard_map/ppermute | solution.py:173
  47.2 6.5 %collective-permute-done.9.refs_3_ = bf16[8,2,64,128]{3,2,1,0:T(8,128)(2,1)S(1)} collective-permute-done((bf16[8,2,64,128]{3,2,1,0:T(8,128)(2,1)S(1)}, bf16[8,2,64,128]{3,2,1,0:T(8,128)(2,1)S(1)}, u32[]{:S(2)}, u32[]{:S(2)}) %collective-permute-start.9) | collective-permute-done | bytes 262176 | tf_op jit(solution)/shard_map/ppermute | solution.py:173
  53.8 1.6 %shard_map.93 = (f32[2,512,128]{2,1,0:T(8,128)S(1)}, bf16[2,512,128]{2,1,0:T(8,128)(2,1)S(1)}, bf16[2,512,128]{2,1,0:T(8,128)(2,1)S(1)}, bf16[2,512,128]{2,1,0:T(8,128)(2,1)S(1)}) custom-call(bf16[8,2,64,128]{3,2,1,0:T(8,128)(2,1)S(1)} %get-tuple-element.29.refs_0_, bf16[8,2,64,128]{3,2,1,0:T(8,128)(2,1)S(1)} %collective-permute-done.7.refs_1_, ...), custom_call_target="tpu_custom_call" | custom-call | flops 1073741824 | bytes 2097152 | tf_op jit(solution)/shard_map/pallas_call | solution.py:269
  55.3 1.8 %collective-permute-start.10 = (bf16[2,512,128]{2,1,0:T(8,128)(2,1)S(1)}, bf16[2,512,128]{2,1,0:T(8,128)(2,1)S(1)}, u32[]{:S(2)}, u32[]{:S(2)}) collective-permute-start(bf16[2,512,128]{2,1,0:T(8,128)(2,1)S(1)} %get-tuple-element.34), channel_id=1, source_target_pairs={{0,1},{1,0},{2,3},{3,2},{4,5},{5,4},{6,7},{7,6},{8,9},{9,8},{10,11... | collective-permute-start | bytes 786440 | tf_op jit(solution)/shard_map/ppermute | solution.py:173
  57.2 0.0 collective-permute-start.11
  57.2 1.7 %collective-permute-start.12 = (bf16[2,512,128]{2,1,0:T(8,128)(2,1)S(1)}, bf16[2,512,128]{2,1,0:T(8,128)(2,1)S(1)}, u32[]{:S(2)}, u32[]{:S(2)}) collective-permute-start(bf16[2,512,128]{2,1,0:T(8,128)(2,1)S(1)} %get-tuple-element.36), channel_id=1, source_target_pairs={{0,3},{1,2},{2,1},{3,0},{4,7},{5,6},{6,5},{7,4},{8,11},{9,10},{10,... | collective-permute-start | bytes 786440 | tf_op jit(solution)/shard_map/ppermute | solution.py:173
  58.9 5.8 %collective-permute-done.10.refs_1_ = bf16[2,512,128]{2,1,0:T(8,128)(2,1)S(1)} collective-permute-done((bf16[2,512,128]{2,1,0:T(8,128)(2,1)S(1)}, bf16[2,512,128]{2,1,0:T(8,128)(2,1)S(1)}, u32[]{:S(2)}, u32[]{:S(2)}) %collective-permute-start.10) | collective-permute-done | bytes 262176 | tf_op jit(solution)/shard_map/ppermute | solution.py:173
  64.7 5.1 %collective-permute-done.11.refs_2_ = bf16[2,512,128]{2,1,0:T(8,128)(2,1)S(1)} collective-permute-done((bf16[2,512,128]{2,1,0:T(8,128)(2,1)S(1)}, bf16[2,512,128]{2,1,0:T(8,128)(2,1)S(1)}, u32[]{:S(2)}, u32[]{:S(2)}) %collective-permute-start.11) | collective-permute-done | bytes 262176 | tf_op jit(solution)/shard_map/ppermute | solution.py:173
  69.7 0.0 collective-permute-done.12.refs_3_
  69.7 1.5 %shard_map.94 = f32[2,4,512,128]{3,2,1,0:T(8,128)} custom-call(f32[2,512,128]{2,1,0:T(8,128)S(1)} %get-tuple-element.33.refs_0_, bf16[2,512,128]{2,1,0:T(8,128)(2,1)S(1)} %collective-permute-done.10.refs_1_, bf16[2,512,128]{2,1,0:T(8,128)(2,1)S(1)} %collective-permute-done.11.refs_2_, bf16[2,512,128]{2,1,0:T(8,128)(2,1)S(1)} %collective-permute-done.12.refs_3_), custom_call_target="tpu_custom_call" | custom-call | tf_op jit(solution)/shard_map/pallas_call | solution.py:293
Async XLA Ops:
  10.9 5.9 %collective-permute-start = (bf16[4,2,64,128]{3,2,1,0:T(8,128)(2,1)}, bf16[4,2,64,128]{3,2,1,0:T(8,128)(2,1)S(1)}, u32[]{:S(2)}, u32[]{:S(2)}) collective-permute-start(bf16[4,2,64,128]{3,2,1,0:T(8,128)(2,1)} %get-tuple-element.22), channel_id=1, source_target_pairs={{0,1},{1,0},{2,3},{3,2},{4,5},{5,4},{6,7},{7,6},{8,9},{9,8},{10,11... | collective-permute-start | bytes 393224 | tf_op jit(solution)/shard_map/ppermute | solution.py:173
  12.4 6.9 %collective-permute-start.1 = (bf16[4,2,64,128]{3,2,1,0:T(8,128)(2,1)}, bf16[4,2,64,128]{3,2,1,0:T(8,128)(2,1)S(1)}, u32[]{:S(2)}, u32[]{:S(2)}) collective-permute-start(bf16[4,2,64,128]{3,2,1,0:T(8,128)(2,1)} %get-tuple-element.23), channel_id=1, source_target_pairs={{0,2},{1,3},{2,0},{3,1},{4,6},{5,7},{6,4},{7,5},{8,10},{9,11},{10,... | collective-permute-start | bytes 393224 | tf_op jit(solution)/shard_map/ppermute | solution.py:173
  13.9 7.6 %collective-permute-start.2 = (bf16[4,2,64,128]{3,2,1,0:T(8,128)(2,1)}, bf16[4,2,64,128]{3,2,1,0:T(8,128)(2,1)S(1)}, u32[]{:S(2)}, u32[]{:S(2)}) collective-permute-start(bf16[4,2,64,128]{3,2,1,0:T(8,128)(2,1)} %get-tuple-element.24), channel_id=1, source_target_pairs={{0,3},{1,2},{2,1},{3,0},{4,7},{5,6},{6,5},{7,4},{8,11},{9,10},{10,... | collective-permute-start | bytes 393224 | tf_op jit(solution)/shard_map/ppermute | solution.py:173
  14.4 7.1 %collective-permute-start.3 = (bf16[4,2,64,128]{3,2,1,0:T(8,128)(2,1)}, bf16[4,2,64,128]{3,2,1,0:T(8,128)(2,1)S(1)}, u32[]{:S(2)}, u32[]{:S(2)}) collective-permute-start(bf16[4,2,64,128]{3,2,1,0:T(8,128)(2,1)} %get-tuple-element.25), channel_id=1, source_target_pairs={{0,4},{1,5},{2,6},{3,7},{4,0},{5,1},{6,2},{7,3},{8,12},{9,13},{10,... | collective-permute-start | bytes 393224 | tf_op jit(solution)/shard_map/ppermute | solution.py:173
  14.4 7.1 %collective-permute-start.4 = (bf16[4,2,64,128]{3,2,1,0:T(8,128)(2,1)}, bf16[4,2,64,128]{3,2,1,0:T(8,128)(2,1)S(1)}, u32[]{:S(2)}, u32[]{:S(2)}) collective-permute-start(bf16[4,2,64,128]{3,2,1,0:T(8,128)(2,1)} %get-tuple-element.26), channel_id=1, source_target_pairs={{0,5},{1,4},{2,7},{3,6},{4,1},{5,0},{6,3},{7,2},{8,13},{9,12},{10,... | collective-permute-start | bytes 393224 | tf_op jit(solution)/shard_map/ppermute | solution.py:173
  16.8 9.6 %collective-permute-start.5 = (bf16[4,2,64,128]{3,2,1,0:T(8,128)(2,1)}, bf16[4,2,64,128]{3,2,1,0:T(8,128)(2,1)S(1)}, u32[]{:S(2)}, u32[]{:S(2)}) collective-permute-start(bf16[4,2,64,128]{3,2,1,0:T(8,128)(2,1)} %get-tuple-element.27), channel_id=1, source_target_pairs={{0,6},{1,7},{2,4},{3,5},{4,2},{5,3},{6,0},{7,1},{8,14},{9,15},{10,... | collective-permute-start | bytes 393224 | tf_op jit(solution)/shard_map/ppermute | solution.py:173
  19.3 7.1 %collective-permute-start.6 = (bf16[4,2,64,128]{3,2,1,0:T(8,128)(2,1)}, bf16[4,2,64,128]{3,2,1,0:T(8,128)(2,1)S(1)}, u32[]{:S(2)}, u32[]{:S(2)}) collective-permute-start(bf16[4,2,64,128]{3,2,1,0:T(8,128)(2,1)} %get-tuple-element.28), channel_id=1, source_target_pairs={{0,7},{1,6},{2,5},{3,4},{4,3},{5,2},{6,1},{7,0},{8,15},{9,14},{10,... | collective-permute-start | bytes 393224 | tf_op jit(solution)/shard_map/ppermute | solution.py:173
  26.3 0.9 %copy-start = (bf16[4,2,64,128]{3,2,1,0:T(8,128)(2,1)S(1)}, bf16[4,2,64,128]{3,2,1,0:T(8,128)(2,1)}, u32[]{:S(2)}) copy-start(bf16[4,2,64,128]{3,2,1,0:T(8,128)(2,1)} %get-tuple-element.21.refs_0_) | copy-start | bytes 393220
  27.3 11.9 %collective-permute-start.7 = (bf16[8,2,64,128]{3,2,1,0:T(8,128)(2,1)S(1)}, bf16[8,2,64,128]{3,2,1,0:T(8,128)(2,1)S(1)}, u32[]{:S(2)}, u32[]{:S(2)}) collective-permute-start(bf16[8,2,64,128]{3,2,1,0:T(8,128)(2,1)S(1)} %get-tuple-element.30), channel_id=1, source_target_pairs={{0,8},{1,9},{2,10},{3,11},{4,12},{5,13},{6,14},{7,15},{8,0},{9,1},... | collective-permute-start | bytes 786440 | tf_op jit(solution)/shard_map/ppermute | solution.py:173
  29.0 18.3 %collective-permute-start.8 = (bf16[8,2,64,128]{3,2,1,0:T(8,128)(2,1)S(1)}, bf16[8,2,64,128]{3,2,1,0:T(8,128)(2,1)S(1)}, u32[]{:S(2)}, u32[]{:S(2)}) collective-permute-start(bf16[8,2,64,128]{3,2,1,0:T(8,128)(2,1)S(1)} %get-tuple-element.31), channel_id=1, source_target_pairs={{0,16},{1,17},{2,18},{3,19},{4,20},{5,21},{6,22},{7,23},{8,24},{9,... | collective-permute-start | bytes 786440 | tf_op jit(solution)/shard_map/ppermute | solution.py:173
  29.3 24.5 %collective-permute-start.9 = (bf16[8,2,64,128]{3,2,1,0:T(8,128)(2,1)S(1)}, bf16[8,2,64,128]{3,2,1,0:T(8,128)(2,1)S(1)}, u32[]{:S(2)}, u32[]{:S(2)}) collective-permute-start(bf16[8,2,64,128]{3,2,1,0:T(8,128)(2,1)S(1)} %get-tuple-element.32), channel_id=1, source_target_pairs={{0,24},{1,25},{2,26},{3,27},{4,28},{5,29},{6,30},{7,31},{8,16},{9,... | collective-permute-start | bytes 786440 | tf_op jit(solution)/shard_map/ppermute | solution.py:173
  55.3 9.3 %collective-permute-start.10 = (bf16[2,512,128]{2,1,0:T(8,128)(2,1)S(1)}, bf16[2,512,128]{2,1,0:T(8,128)(2,1)S(1)}, u32[]{:S(2)}, u32[]{:S(2)}) collective-permute-start(bf16[2,512,128]{2,1,0:T(8,128)(2,1)S(1)} %get-tuple-element.34), channel_id=1, source_target_pairs={{0,1},{1,0},{2,3},{3,2},{4,5},{5,4},{6,7},{7,6},{8,9},{9,8},{10,11... | collective-permute-start | bytes 786440 | tf_op jit(solution)/shard_map/ppermute | solution.py:173
  57.2 12.6 %collective-permute-start.11 = (bf16[2,512,128]{2,1,0:T(8,128)(2,1)S(1)}, bf16[2,512,128]{2,1,0:T(8,128)(2,1)S(1)}, u32[]{:S(2)}, u32[]{:S(2)}) collective-permute-start(bf16[2,512,128]{2,1,0:T(8,128)(2,1)S(1)} %get-tuple-element.35), channel_id=1, source_target_pairs={{0,2},{1,3},{2,0},{3,1},{4,6},{5,7},{6,4},{7,5},{8,10},{9,11},{10,... | collective-permute-start | bytes 786440 | tf_op jit(solution)/shard_map/ppermute | solution.py:173
  57.2 12.6 %collective-permute-start.12 = (bf16[2,512,128]{2,1,0:T(8,128)(2,1)S(1)}, bf16[2,512,128]{2,1,0:T(8,128)(2,1)S(1)}, u32[]{:S(2)}, u32[]{:S(2)}) collective-permute-start(bf16[2,512,128]{2,1,0:T(8,128)(2,1)S(1)} %get-tuple-element.36), channel_id=1, source_target_pairs={{0,3},{1,2},{2,1},{3,0},{4,7},{5,6},{6,5},{7,4},{8,11},{9,10},{10,... | collective-permute-start | bytes 786440 | tf_op jit(solution)/shard_map/ppermute | solution.py:173

commit v2 on v1

v2 whole, which is shorter than its diff:
```python
import functools
import math

import jax
import jax.numpy as jnp
import ml_dtypes
import numpy as np
from jax import lax
from jax.experimental import pallas as pl
from jax.experimental.pallas import tpu as pltpu
from jax.sharding import PartitionSpec as P

REFLECTIVITY = 0.6
LANES = 128
BLOCK = 16
SPECTRUM_VMEM = 60 * 2**20
REGROUP_VMEM = 16 * 2**20
PRODUCT_VMEM = 24 * 2**20
COLLECT_VMEM = 16 * 2**20


def split_pair(values):
    high = values.astype(ml_dtypes.bfloat16)
    low = (values - high.astype(np.float64)).astype(ml_dtypes.bfloat16)
    return high, low


@functools.lru_cache(maxsize=None)
def tables(samples, taps, bins):
    bin_index = np.arange(1, bins + 1)[:, None]
    unit = 2.0 * math.pi / samples
    time_angle = (bin_index * np.arange(samples)[None] % samples) * unit
    head = samples - taps
    factor = 1.0 / math.sqrt(samples)
    twiddle = np.concatenate([np.cos(time_angle), -np.sin(time_angle)])
    head_high, head_low = split_pair(twiddle[:, :head])
    head_table = np.concatenate([head_high, head_low])
    tap_table = (twiddle[:, :taps] * factor).astype(np.float32)
    turn_table = twiddle[:, head:].astype(np.float32)
    lane = np.arange(taps)
    prefix = (lane[:, None] <= taps - 1 - lane[None]).astype(ml_dtypes.bfloat16)
    delay_angle = (bin_index * np.arange(LANES)[None] % samples) * unit
    gain = 1.0 / (1.0 - REFLECTIVITY * np.exp(-1j * delay_angle))
    gain[:, LANES - 1] = 0.0
    gain_table = np.concatenate([gain.real, gain.imag]).astype(np.float32)
    return head_table, tap_table, turn_table, prefix, gain_table


def halves(value):
    high = value.astype(jnp.bfloat16)
    low = (value - high.astype(jnp.float32)).astype(jnp.bfloat16)
    return jnp.concatenate([high, low])


def nt_dot(left, right):
    return lax.dot_general(
        left, right, (((1,), (1,)), ((), ())), preferred_element_type=jnp.float32
    )


def spectrum_body(place, bins, head_ref, tap_ref, turn_ref, prefix_ref, gain_ref, sig_ref, delay_ref, dead_ref, rec_ref, *rest):
    out_refs, rows_ref = rest[:-1], rest[-1]
    shots, receivers, samples = rec_ref.shape
    head = head_ref.shape[1]
    both = 2 * bins
    pulses = sig_ref[...].astype(jnp.float32)
    tap_table = tap_ref[...]
    parts = [halves(tap_table * pulses[shot : shot + 1]) for shot in range(shots)]
    sums = jnp.dot(
        jnp.concatenate(parts), prefix_ref[...], preferred_element_type=jnp.float32
    )
    turn_real, turn_imag = turn_ref[:bins], turn_ref[bins:]
    traces = rec_ref[...].reshape(shots * receivers, samples)
    whole = nt_dot(head_ref[...], traces[:, :head])
    whole = whole[:both] + whole[both:]
    lookup = jnp.where(dead_ref[...] != 0, LANES - 1, delay_ref[...])
    gain_table = gain_ref[...]
    for shot in range(shots):
        base = shot * 2 * both
        filt = sums[base : base + both] + sums[base + both : base + 2 * both]
        filt_real, filt_imag = filt[:bins], filt[bins:]
        tail_filter = jnp.concatenate(
            [
                filt_real * turn_real - filt_imag * turn_imag,
                filt_real * turn_imag + filt_imag * turn_real,
            ]
        )
        columns = slice(shot * receivers, (shot + 1) * receivers)
        tail = nt_dot(halves(tail_filter), traces[columns, head:])
        tail = tail[:both] + tail[both:]
        main_real, main_imag = whole[:bins, columns], whole[bins:, columns]
        pulse_real, pulse_imag = filt_real[:, :1], filt_imag[:, :1]
        real = main_real * pulse_real - main_imag * pulse_imag + tail[:bins]
        imag = main_real * pulse_imag + main_imag * pulse_real + tail[bins:]
        index = jnp.broadcast_to(lookup[shot : shot + 1], (both, receivers))
        gain = jnp.take_along_axis(gain_table, index, axis=1)
        gain_real, gain_imag = gain[:bins], gain[bins:]
        rows_ref[:bins, shot] = real * gain_real - imag * gain_imag
        rows_ref[bins:, shot] = real * gain_imag + imag * gain_real
    place(rows_ref, out_refs)


def spectrum_call(recorded, signatures, ghost_delay, dead_trace, bins, place, out_shapes, out_specs, first, count, block):
    samples, taps, receivers = recorded.shape[2], signatures.shape[1], recorded.shape[1]
    constants = [jnp.asarray(t) for t in tables(samples, taps, bins)]
    fixed = [pl.BlockSpec(t.shape, lambda i: (0, 0), pipeline_mode=pl.Buffered(1)) for t in constants]
    start = first // block
    rows = lambda width: pl.BlockSpec((block, width), lambda i: (i + start, 0))
    return pl.pallas_call(
        functools.partial(spectrum_body, place, bins),
        grid=(count // block,),
        in_specs=fixed
        + [rows(taps), rows(receivers), rows(receivers), pl.BlockSpec((block, receivers, samples), lambda i: (i + start, 0, 0))],
        out_specs=out_specs,
        out_shape=out_shapes,
        scratch_shapes=[pltpu.VMEM((2 * bins, block, receivers), jnp.float32)],
        compiler_params=pltpu.CompilerParams(vmem_limit_bytes=SPECTRUM_VMEM),
        cost_estimate=pl.CostEstimate(flops=2 * 2 * count * receivers * samples * 4 * bins // 2, bytes_accessed=count * receivers * samples * 2, transcendentals=0),
    )(*constants, signatures, ghost_delay, dead_trace, recorded)


def axis_sizes():
    return lax.axis_size("freq"), lax.axis_size("section"), lax.axis_size("rcv")


def place_plain(rows_ref, out_refs):
    (out_ref,) = out_refs
    bins = out_ref.shape[0]
    for part in range(2):
        out_ref[:, part] = rows_ref[part * bins : (part + 1) * bins].astype(out_ref.dtype)


def exchange(array, across):
    if not across:
        return array
    return lax.ppermute(array, "rcv", [(c, c ^ across) for c in range(lax.axis_size("rcv"))])


def in_vmem(count):
    return [pl.BlockSpec(memory_space=pltpu.VMEM)] * count


def product_body(in_ref, *refs):
    groups = lax.axis_size("rcv")
    left_ref, out_refs = refs[-1], refs[:-1]
    stations = left_ref.shape[0]
    sources, _, shots, receivers = in_ref.shape
    for source in range(sources):
        rows = pl.ds(source // groups * shots, shots)
        for part in range(2):
            columns = pl.ds(source % groups * receivers + part * stations, receivers)
            left_ref[rows, columns] = in_ref[source, part]
    left = left_ref[...]
    scale = 1.0 / math.sqrt(stations)
    mine = lax.axis_index("rcv")
    for across in reversed(range(groups)):
        column = pl.multiple_of((mine ^ across) * receivers, receivers)
        real = left_ref[:, pl.ds(column, receivers)]
        imag = left_ref[:, pl.ds(pl.multiple_of(column + stations, receivers), receivers)]
        right = jnp.concatenate(
            [jnp.concatenate([real, imag], axis=1), jnp.concatenate([-imag, real], axis=1)]
        )
        both = jnp.dot(left, right, preferred_element_type=jnp.float32) * scale
        out_ref = out_refs[across]
        out_ref[0] = both[:, :receivers].astype(out_ref.dtype)
        out_ref[1] = both[:, receivers:].astype(out_ref.dtype)


def product(array):
    groups, receivers = lax.axis_size("rcv"), array.shape[3]
    stations = groups * receivers
    return pl.pallas_call(
        product_body,
        out_shape=[
            jax.ShapeDtypeStruct((2, stations, receivers), jnp.bfloat16 if across else jnp.float32)
            for across in range(groups)
        ],
        in_specs=in_vmem(1),
        out_specs=in_vmem(groups),
        scratch_shapes=[pltpu.VMEM((stations, 2 * stations), jnp.bfloat16)],
        compiler_params=pltpu.CompilerParams(vmem_limit_bytes=PRODUCT_VMEM),
        cost_estimate=pl.CostEstimate(flops=8 * stations**3, bytes_accessed=8 * stations**2, transcendentals=0),
    )(array)


def collect_body(*refs):
    in_refs, out_ref = refs[:-1], refs[-1]
    mine = lax.axis_index("rcv")
    for across, ref in enumerate(in_refs):
        for part in range(2):
            out_ref[part, mine ^ across] = ref[part].astype(out_ref.dtype)


def collect(arrays):
    parts, stations, receivers = arrays[0].shape
    return pl.pallas_call(
        collect_body,
        out_shape=jax.ShapeDtypeStruct((parts, len(arrays), stations, receivers), jnp.float32),
        in_specs=in_vmem(len(arrays)),
        out_specs=pl.BlockSpec(memory_space=pltpu.VMEM),
        compiler_params=pltpu.CompilerParams(vmem_limit_bytes=COLLECT_VMEM),
    )(*arrays)


def spectra(recorded, signatures, ghost_delay, dead_trace):
    shots, receivers, _ = recorded.shape
    bins = math.prod(axis_sizes())
    block = min(shots, BLOCK)
    (deghosted,) = spectrum_call(
        recorded,
        signatures,
        ghost_delay,
        dead_trace,
        bins,
        place_plain,
        [jax.ShapeDtypeStruct((bins, 2, shots, receivers), jnp.bfloat16)],
        [pl.BlockSpec((bins, 2, block, receivers), lambda i: (0, 0, i, 0))],
        0,
        shots,
        block,
    )
    return deghosted


def per_device(recorded, signatures, ghost_delay, dead_trace):
    deghosted = spectra(recorded, signatures, ghost_delay, dead_trace)
    axes = ("freq", "section", "rcv")
    relayed = lax.all_to_all(deghosted, axes, split_axis=0, concat_axis=0, tiled=True)
    return collect([exchange(b, across) for across, b in enumerate(product(relayed))])


def solution(mesh):
    return jax.shard_map(
        per_device,
        mesh=mesh,
        in_specs=(
            P(("line", "freq", "section"), "rcv", None),
            P(("line", "freq", "section"), None),
            P(("line", "freq", "section"), "rcv"),
            P(("line", "freq", "section"), "rcv"),
        ),
        out_specs=P(None, ("freq", "section"), "line", "rcv"),
        check_vma=False,
    )
```

time: 71.4 us -> 62.9 us (0.88)
  the two profiles are of different devices: /device:TPU:16 before, /device:TPU:0 now
where the time goes in v2:
time: 62.9 us; the launch traced here: 62.6 us
  blocking collectives  33.7 us (54%)
  Pallas kernels  13.8 us (22%)
  waiting for transfers between devices  11.5 us (18%)
  starting transfers between devices  3.55 us (6%)
    all_to_all x1, blocking collectives, per_device(): lax.all_to_all(deghosted, axes, split_axis=0, concat_axis=0, tiled=True)  33.7 us
    ppermute x3, waiting for transfers between devices, exchange(): lax.ppermute(array, 'rcv', [(c, c ^ across) for c in range(lax.axis_size(...  11.5 us
    pallas_call x1, Pallas kernels, spectrum_call(): pl.pallas_call(functools.partial(spectrum_body, place, bins), grid=(count...  10.8 us
    ppermute x3, starting transfers between devices, exchange(): lax.ppermute(array, 'rcv', [(c, c ^ across) for c in range(lax.axis_size(...  3.55 us
    pallas_call x1, Pallas kernels, product(): pl.pallas_call(product_body, out_shape=[jax.ShapeDtypeStruct((2, stations...  1.54 us
    pallas_call x1, Pallas kernels, collect(): pl.pallas_call(collect_body, out_shape=jax.ShapeDtypeStruct((parts, len(a...  1.46 us
  transfers between devices with their start and end apart: 3, of which 3 were waited for; matrix products, arithmetic and copies ran while one was open for 0% of the time, Pallas kernels for 0%

profile of v2, /device:TPU:0, one launch (start us, length us, event | category | flops | bytes accessed | tf_op | source)
XLA Modules:
  0.0 62.6 jit_solution(3258897633468560074)
XLA Ops:
  0.0 10.8 %shard_map.91 = bf16[32,2,64,128]{3,2,1,0:T(8,128)(2,1)} custom-call(bf16[128,768]{1,0:T(8,128)(2,1)} %constant.10.clone.head_ref, f32[64,256]{1,0:T(8,128)} %constant.11.clone.tap_ref, f32[64,256]{1,0:T(8,128)} %constant.12.clone.turn_ref, bf16[256,256]{1,0:T(8,128)(2,1)} %constant.13.clone.prefix_ref, f32[64,128]{1,0:T(8,128)} %constant.14.clone.gain_ref, ...), custom_call_target="tpu_custom_call" | custom-call | flops 2147483648 | bytes 16777216 | tf_op jit(solution)/shard_map/pallas_call | solution.py:109
  10.8 33.7 %all_to_all.5.in_ref = bf16[32,2,64,128]{3,2,1,0:T(8,128)(2,1)S(1)} all-to-all(bf16[32,2,64,128]{3,2,1,0:T(8,128)(2,1)} %shard_map.91), channel_id=1, replica_groups=mesh['line'=1,'freq'=4,'section'=2,'rcv'=4] {'freq','section','rcv'}, dimensions={0} | all-to-all | bytes 2097152 | tf_op jit(solution)/shard_map/all_to_all | solution.py:228
  44.6 1.5 %shard_map.92 = (f32[2,512,128]{2,1,0:T(8,128)S(1)}, bf16[2,512,128]{2,1,0:T(8,128)(2,1)S(1)}, bf16[2,512,128]{2,1,0:T(8,128)(2,1)S(1)}, bf16[2,512,128]{2,1,0:T(8,128)(2,1)S(1)}) custom-call(bf16[32,2,64,128]{3,2,1,0:T(8,128)(2,1)S(1)} %all_to_all.5.in_ref), custom_call_target="tpu_custom_call" | custom-call | flops 1073741824 | bytes 2097152 | tf_op jit(solution)/shard_map/pallas_call | solution.py:172
  46.1 1.4 %collective-permute-start = (bf16[2,512,128]{2,1,0:T(8,128)(2,1)S(1)}, bf16[2,512,128]{2,1,0:T(8,128)(2,1)S(1)}, u32[]{:S(2)}, u32[]{:S(2)}) collective-permute-start(bf16[2,512,128]{2,1,0:T(8,128)(2,1)S(1)} %get-tuple-element.10), channel_id=1, source_target_pairs={{0,1},{1,0},{2,3},{3,2},{4,5},{5,4},{6,7},{7,6},{8,9},{9,8},{10,11... | collective-permute-start | bytes 786440 | tf_op jit(solution)/shard_map/ppermute | solution.py:136
  47.5 1.5 %collective-permute-start.1 = (bf16[2,512,128]{2,1,0:T(8,128)(2,1)S(1)}, bf16[2,512,128]{2,1,0:T(8,128)(2,1)S(1)}, u32[]{:S(2)}, u32[]{:S(2)}) collective-permute-start(bf16[2,512,128]{2,1,0:T(8,128)(2,1)S(1)} %get-tuple-element.11), channel_id=1, source_target_pairs={{0,2},{1,3},{2,0},{3,1},{4,6},{5,7},{6,4},{7,5},{8,10},{9,11},{10,... | collective-permute-start | bytes 786440 | tf_op jit(solution)/shard_map/ppermute | solution.py:136
  49.0 0.7 %collective-permute-start.2 = (bf16[2,512,128]{2,1,0:T(8,128)(2,1)S(1)}, bf16[2,512,128]{2,1,0:T(8,128)(2,1)S(1)}, u32[]{:S(2)}, u32[]{:S(2)}) collective-permute-start(bf16[2,512,128]{2,1,0:T(8,128)(2,1)S(1)} %get-tuple-element.12), channel_id=1, source_target_pairs={{0,3},{1,2},{2,1},{3,0},{4,7},{5,6},{6,5},{7,4},{8,11},{9,10},{10,... | collective-permute-start | bytes 786440 | tf_op jit(solution)/shard_map/ppermute | solution.py:136
  49.7 5.7 %collective-permute-done.refs_1_ = bf16[2,512,128]{2,1,0:T(8,128)(2,1)S(1)} collective-permute-done((bf16[2,512,128]{2,1,0:T(8,128)(2,1)S(1)}, bf16[2,512,128]{2,1,0:T(8,128)(2,1)S(1)}, u32[]{:S(2)}, u32[]{:S(2)}) %collective-permute-start) | collective-permute-done | bytes 262176 | tf_op jit(solution)/shard_map/ppermute | solution.py:136
  55.4 4.1 %collective-permute-done.1.refs_2_ = bf16[2,512,128]{2,1,0:T(8,128)(2,1)S(1)} collective-permute-done((bf16[2,512,128]{2,1,0:T(8,128)(2,1)S(1)}, bf16[2,512,128]{2,1,0:T(8,128)(2,1)S(1)}, u32[]{:S(2)}, u32[]{:S(2)}) %collective-permute-start.1) | collective-permute-done | bytes 262176 | tf_op jit(solution)/shard_map/ppermute | solution.py:136
  59.5 1.7 %collective-permute-done.2.refs_3_ = bf16[2,512,128]{2,1,0:T(8,128)(2,1)S(1)} collective-permute-done((bf16[2,512,128]{2,1,0:T(8,128)(2,1)S(1)}, bf16[2,512,128]{2,1,0:T(8,128)(2,1)S(1)}, u32[]{:S(2)}, u32[]{:S(2)}) %collective-permute-start.2) | collective-permute-done | bytes 262176 | tf_op jit(solution)/shard_map/ppermute | solution.py:136
  61.2 1.5 %shard_map.93 = f32[2,4,512,128]{3,2,1,0:T(8,128)} custom-call(f32[2,512,128]{2,1,0:T(8,128)S(1)} %get-tuple-element.9.refs_0_, bf16[2,512,128]{2,1,0:T(8,128)(2,1)S(1)} %collective-permute-done.refs_1_, bf16[2,512,128]{2,1,0:T(8,128)(2,1)S(1)} %collective-permute-done.1.refs_2_, bf16[2,512,128]{2,1,0:T(8,128)(2,1)S(1)} %collective-permute-done.2.refs_3_), custom_call_target="tpu_custom_call" | custom-call | tf_op jit(solution)/shard_map/pallas_call | solution.py:196
Async XLA Ops:
  46.1 9.3 %collective-permute-start = (bf16[2,512,128]{2,1,0:T(8,128)(2,1)S(1)}, bf16[2,512,128]{2,1,0:T(8,128)(2,1)S(1)}, u32[]{:S(2)}, u32[]{:S(2)}) collective-permute-start(bf16[2,512,128]{2,1,0:T(8,128)(2,1)S(1)} %get-tuple-element.10), channel_id=1, source_target_pairs={{0,1},{1,0},{2,3},{3,2},{4,5},{5,4},{6,7},{7,6},{8,9},{9,8},{10,11... | collective-permute-start | bytes 786440 | tf_op jit(solution)/shard_map/ppermute | solution.py:136
  47.5 12.0 %collective-permute-start.1 = (bf16[2,512,128]{2,1,0:T(8,128)(2,1)S(1)}, bf16[2,512,128]{2,1,0:T(8,128)(2,1)S(1)}, u32[]{:S(2)}, u32[]{:S(2)}) collective-permute-start(bf16[2,512,128]{2,1,0:T(8,128)(2,1)S(1)} %get-tuple-element.11), channel_id=1, source_target_pairs={{0,2},{1,3},{2,0},{3,1},{4,6},{5,7},{6,4},{7,5},{8,10},{9,11},{10,... | collective-permute-start | bytes 786440 | tf_op jit(solution)/shard_map/ppermute | solution.py:136
  49.0 12.2 %collective-permute-start.2 = (bf16[2,512,128]{2,1,0:T(8,128)(2,1)S(1)}, bf16[2,512,128]{2,1,0:T(8,128)(2,1)S(1)}, u32[]{:S(2)}, u32[]{:S(2)}) collective-permute-start(bf16[2,512,128]{2,1,0:T(8,128)(2,1)S(1)} %get-tuple-element.12), channel_id=1, source_target_pairs={{0,3},{1,2},{2,1},{3,0},{4,7},{5,6},{6,5},{7,4},{8,11},{9,10},{10,... | collective-permute-start | bytes 786440 | tf_op jit(solution)/shard_map/ppermute | solution.py:136

commit v3 on v2

v3 whole, which is shorter than its diff:
```python
import functools
import math

import jax
import jax.numpy as jnp
import ml_dtypes
import numpy as np
from jax import lax
from jax.experimental import pallas as pl
from jax.experimental.pallas import tpu as pltpu
from jax.sharding import PartitionSpec as P

REFLECTIVITY = 0.6
LANES = 128
BLOCK = 16
ORDER = (3, 2, 1)
SPECTRUM_VMEM = 56 * 2**20
REGROUP_VMEM = 16 * 2**20
PRODUCT_VMEM = 24 * 2**20
COLLECT_VMEM = 16 * 2**20


def split_pair(values):
    high = values.astype(ml_dtypes.bfloat16)
    low = (values - high.astype(np.float64)).astype(ml_dtypes.bfloat16)
    return high, low


@functools.lru_cache(maxsize=None)
def tables(samples, taps, bins):
    bin_index = np.arange(1, bins + 1)[:, None]
    unit = 2.0 * math.pi / samples
    time_angle = (bin_index * np.arange(samples)[None] % samples) * unit
    head = samples - taps
    factor = 1.0 / math.sqrt(samples)
    twiddle = np.concatenate([np.cos(time_angle), -np.sin(time_angle)])
    head_high, head_low = split_pair(twiddle[:, :head])
    head_table = np.concatenate([head_high, head_low])
    tap_table = (twiddle[:, :taps] * factor).astype(np.float32)
    turn_table = twiddle[:, head:].astype(np.float32)
    lane = np.arange(taps)
    prefix = (lane[:, None] <= taps - 1 - lane[None]).astype(ml_dtypes.bfloat16)
    delay_angle = (bin_index * np.arange(LANES)[None] % samples) * unit
    gain = 1.0 / (1.0 - REFLECTIVITY * np.exp(-1j * delay_angle))
    gain[:, LANES - 1] = 0.0
    gain_table = np.concatenate([gain.real, gain.imag]).astype(np.float32)
    return head_table, tap_table, turn_table, prefix, gain_table


def halves(value):
    high = value.astype(jnp.bfloat16)
    low = (value - high.astype(jnp.float32)).astype(jnp.bfloat16)
    return jnp.concatenate([high, low])


def nt_dot(left, right):
    return lax.dot_general(
        left, right, (((1,), (1,)), ((), ())), preferred_element_type=jnp.float32
    )


def spectrum_body(bins, chunk, *refs):
    tables_count = 5
    hbm_refs, out_ref = refs[: tables_count + 4], refs[tables_count + 4]
    buffers, sems = refs[tables_count + 5 : -2], refs[-2]
    rows_ref = refs[-1]
    head_ref, tap_ref, turn_ref, prefix_ref, gain_ref, sig_ref, delay_ref, dead_ref, rec_ref = buffers
    shots, receivers, samples = rec_ref.shape
    steps = shots // chunk
    small = len(hbm_refs) - 1

    def small_copy(i):
        return pltpu.make_async_copy(hbm_refs[i], buffers[i], sems.at[i])

    def trace_copy(step):
        span = pl.ds(step * chunk, chunk)
        return pltpu.make_async_copy(hbm_refs[small].at[span], rec_ref.at[span], sems.at[small + step])

    for i in range(small):
        small_copy(i).start()
    for step in range(steps):
        trace_copy(step).start()
    for i in range(small):
        small_copy(i).wait()

    head = head_ref.shape[1]
    both = 2 * bins
    turn_real, turn_imag = turn_ref[:bins], turn_ref[bins:]

    def one_step(step, carry):
        trace_copy(step).wait()
        first = pl.multiple_of(step * chunk, chunk)
        pulses = sig_ref[pl.ds(first, chunk), :].astype(jnp.float32)
        tap_table = tap_ref[...]
        parts = [halves(tap_table * pulses[shot : shot + 1]) for shot in range(chunk)]
        sums = jnp.dot(
            jnp.concatenate(parts), prefix_ref[...], preferred_element_type=jnp.float32
        )
        span = pl.ds(first, chunk)
        lookup = jnp.where(dead_ref[span, :] != 0, LANES - 1, delay_ref[span, :])
        for shot in range(chunk):
            traces = rec_ref[first + shot]
            main = nt_dot(head_ref[...], traces[:, :head])
            main = main[:both] + main[both:]
            base = shot * 2 * both
            filt = sums[base : base + both] + sums[base + both : base + 2 * both]
            filt_real, filt_imag = filt[:bins], filt[bins:]
            tail_filter = jnp.concatenate(
                [
                    filt_real * turn_real - filt_imag * turn_imag,
                    filt_real * turn_imag + filt_imag * turn_real,
                ]
            )
            tail = nt_dot(halves(tail_filter), traces[:, head:])
            tail = tail[:both] + tail[both:]
            main_real, main_imag = main[:bins], main[bins:]
            pulse_real, pulse_imag = filt_real[:, :1], filt_imag[:, :1]
            real = main_real * pulse_real - main_imag * pulse_imag + tail[:bins]
            imag = main_real * pulse_imag + main_imag * pulse_real + tail[bins:]
            index = jnp.broadcast_to(lookup[shot : shot + 1], (both, receivers))
            gain = jnp.take_along_axis(gain_ref[...], index, axis=1)
            gain_real, gain_imag = gain[:bins], gain[bins:]
            rows_ref[:bins, shot] = real * gain_real - imag * gain_imag
            rows_ref[bins:, shot] = real * gain_imag + imag * gain_real
        for part in range(2):
            rows = rows_ref[part * bins : (part + 1) * bins]
            out_ref[:, part, span, :] = rows.astype(out_ref.dtype)
        return carry

    lax.fori_loop(0, steps, one_step, 0)


def spectra(recorded, signatures, ghost_delay, dead_trace):
    shots, receivers, samples = recorded.shape
    taps = signatures.shape[1]
    bins = math.prod(axis_sizes())
    chunk = min(shots, BLOCK)
    constants = [jnp.asarray(t) for t in tables(samples, taps, bins)]
    operands = (*constants, signatures, ghost_delay, dead_trace, recorded)
    return pl.pallas_call(
        functools.partial(spectrum_body, bins, chunk),
        in_specs=[pl.BlockSpec(memory_space=pl.ANY)] * len(operands),
        out_specs=pl.BlockSpec(memory_space=pltpu.VMEM),
        out_shape=jax.ShapeDtypeStruct((bins, 2, shots, receivers), jnp.bfloat16),
        scratch_shapes=[pltpu.VMEM(x.shape, x.dtype) for x in operands]
        + [
            pltpu.SemaphoreType.DMA((len(operands) - 1 + shots // chunk,)),
            pltpu.VMEM((2 * bins, chunk, receivers), jnp.float32),
        ],
        compiler_params=pltpu.CompilerParams(vmem_limit_bytes=SPECTRUM_VMEM),
        cost_estimate=pl.CostEstimate(
            flops=8 * bins * recorded.size, bytes_accessed=2 * recorded.size, transcendentals=0
        ),
    )(*operands)


def axis_sizes():
    return lax.axis_size("freq"), lax.axis_size("section"), lax.axis_size("rcv")


def exchange(array, across):
    if not across:
        return array
    return lax.ppermute(array, "rcv", [(c, c ^ across) for c in range(lax.axis_size("rcv"))])


def in_vmem(count):
    return [pl.BlockSpec(memory_space=pltpu.VMEM)] * count


def own_columns(part_ref, across):
    stations = part_ref.shape[0]
    receivers = stations // lax.axis_size("rcv")
    column = (lax.axis_index("rcv") ^ across) * receivers
    return part_ref[:, pl.ds(pl.multiple_of(column, receivers), receivers)]


def block_product(real_ref, imag_ref, across):
    stations = real_ref.shape[0]
    real, imag = own_columns(real_ref, across), own_columns(imag_ref, across)
    right = jnp.concatenate(
        [jnp.concatenate([real, imag], axis=1), jnp.concatenate([-imag, real], axis=1)]
    )
    left = jnp.concatenate([real_ref[...], imag_ref[...]], axis=1)
    both = jnp.dot(left, right, preferred_element_type=jnp.float32)
    both = both * (1.0 / math.sqrt(stations))
    receivers = real.shape[1]
    return both[:, :receivers], both[:, receivers:]


def first_product_body(in_ref, real_ref, imag_ref, out_ref):
    groups = lax.axis_size("rcv")
    sources, _, shots, receivers = in_ref.shape
    for source in range(sources):
        rows = pl.ds(source // groups * shots, shots)
        columns = pl.ds(source % groups * receivers, receivers)
        real_ref[rows, columns] = in_ref[source, 0]
        imag_ref[rows, columns] = in_ref[source, 1]
    for part, block in enumerate(block_product(real_ref, imag_ref, ORDER[0])):
        out_ref[part] = block.astype(out_ref.dtype)


def other_product_body(real_ref, imag_ref, *out_refs):
    for across, out_ref in zip(ORDER[1:], out_refs, strict=True):
        for part, block in enumerate(block_product(real_ref, imag_ref, across)):
            out_ref[part] = block.astype(out_ref.dtype)


def own_product_body(real_ref, imag_ref, result_ref, own_ref, sems):
    mine = lax.axis_index("rcv")
    copies = []
    for part, block in enumerate(block_product(real_ref, imag_ref, 0)):
        own_ref[part] = block
        copy = pltpu.make_async_copy(
            own_ref.at[part], result_ref.at[part, mine], sems.at[part]
        )
        copy.start()
        copies.append(copy)
    for copy in copies:
        copy.wait()


def collect_body(offsets, *refs):
    in_refs, (result_ref, wide_ref, sems) = refs[: len(offsets)], refs[-3:]
    mine = lax.axis_index("rcv")
    copies = []
    for i, (across, in_ref) in enumerate(zip(offsets, in_refs, strict=True)):
        for part in range(2):
            wide_ref[i, part] = in_ref[part].astype(jnp.float32)
            copy = pltpu.make_async_copy(
                wide_ref.at[i, part], result_ref.at[part, mine ^ across], sems.at[i, part]
            )
            copy.start()
            copies.append(copy)
    for copy in copies:
        copy.wait()


def collect(arrays, offsets, result):
    anywhere = pl.BlockSpec(memory_space=pl.ANY)
    count, size = len(arrays), arrays[0].size
    return pl.pallas_call(
        functools.partial(collect_body, offsets),
        out_shape=jax.ShapeDtypeStruct(result.shape, result.dtype),
        in_specs=in_vmem(count) + [anywhere],
        out_specs=anywhere,
        scratch_shapes=[
            pltpu.VMEM((count,) + arrays[0].shape, jnp.float32),
            pltpu.SemaphoreType.DMA((count, 2)),
        ],
        input_output_aliases={count: 0},
        compiler_params=pltpu.CompilerParams(vmem_limit_bytes=COLLECT_VMEM),
        cost_estimate=pl.CostEstimate(flops=0, bytes_accessed=6 * count * size, transcendentals=0),
    )(*arrays, result)


def products(array):
    groups, receivers = lax.axis_size("rcv"), array.shape[3]
    stations = groups * receivers
    matrix = jax.ShapeDtypeStruct((stations, stations), jnp.bfloat16)
    block = jax.ShapeDtypeStruct((2, stations, receivers), jnp.bfloat16)

    def options(count):
        return {
            "compiler_params": pltpu.CompilerParams(vmem_limit_bytes=PRODUCT_VMEM),
            "cost_estimate": pl.CostEstimate(
                flops=8 * count * stations**2 * receivers,
                bytes_accessed=4 * stations**2,
                transcendentals=0,
            ),
        }

    real, imag, first = pl.pallas_call(
        first_product_body,
        out_shape=[matrix, matrix, block],
        in_specs=in_vmem(1),
        out_specs=in_vmem(3),
        **options(1),
    )(array)
    others = pl.pallas_call(
        other_product_body,
        out_shape=[block] * (groups - 2),
        in_specs=in_vmem(2),
        out_specs=in_vmem(groups - 2),
        **options(groups - 2),
    )(real, imag)
    own = pl.pallas_call(
        own_product_body,
        out_shape=jax.ShapeDtypeStruct((2, groups, stations, receivers), jnp.float32),
        in_specs=in_vmem(2),
        out_specs=pl.BlockSpec(memory_space=pl.ANY),
        scratch_shapes=[
            pltpu.VMEM((2, stations, receivers), jnp.float32),
            pltpu.SemaphoreType.DMA((2,)),
        ],
        **options(1),
    )(real, imag)
    return [first, *others], own


def per_device(recorded, signatures, ghost_delay, dead_trace):
    deghosted = spectra(recorded, signatures, ghost_delay, dead_trace)
    axes = ("freq", "section", "rcv")
    relayed = lax.all_to_all(deghosted, axes, split_axis=0, concat_axis=0, tiled=True)
    blocks, result = products(relayed)
    arrived = [exchange(block, across) for across, block in zip(ORDER, blocks, strict=True)]
    result = collect(arrived[:1], ORDER[:1], result)
    return collect(arrived[1:], ORDER[1:], result)


def solution(mesh):
    return jax.shard_map(
        per_device,
        mesh=mesh,
        in_specs=(
            P(("line", "freq", "section"), "rcv", None),
            P(("line", "freq", "section"), None),
            P(("line", "freq", "section"), "rcv"),
            P(("line", "freq", "section"), "rcv"),
        ),
        out_specs=P(None, ("freq", "section"), "line", "rcv"),
        check_vma=False,
    )
```

time: 62.9 us -> 61.1 us (0.971)
  waiting for transfers between devices: 11.5 us -> 8.65 us
  Pallas kernels: 13.8 us -> 14.8 us
    ppermute x3, waiting for transfers between devices: 11.5 us -> 8.65 us  [exchange(): lax.ppermute(array, 'rcv', [(c, c ^ across) for c in range(lax.axis_size(...]
    pallas_call x3 -> x6, Pallas kernels: 13.8 us -> 14.8 us  [the longest x1 10.4 us: spectra(): pl.pallas_call(functools.partial(spectrum_body, bins, chunk), in_specs=[p...]
  transfers between devices with their start and end apart: 3 -> 3, of which waited for: 3 -> 3; matrix products, arithmetic and copies ran while one was open for 0% -> 0% of each run, Pallas kernels for 0% -> 5%
where the time goes in v3:
time: 61.1 us; the launch traced here: 60.9 us
  blocking collectives  33.7 us (55%)
  Pallas kernels  14.8 us (24%)
  waiting for transfers between devices  8.65 us (14%)
  starting transfers between devices  3.62 us (6%)
    all_to_all x1, blocking collectives, per_device(): lax.all_to_all(deghosted, axes, split_axis=0, concat_axis=0, tiled=True)  33.7 us
    pallas_call x1, Pallas kernels, spectra(): pl.pallas_call(functools.partial(spectrum_body, bins, chunk), in_specs=[p...  10.4 us
    ppermute x3, waiting for transfers between devices, exchange(): lax.ppermute(array, 'rcv', [(c, c ^ across) for c in range(lax.axis_size(...  8.65 us
    ppermute x3, starting transfers between devices, exchange(): lax.ppermute(array, 'rcv', [(c, c ^ across) for c in range(lax.axis_size(...  3.62 us
    pallas_call x2, Pallas kernels, collect(): pl.pallas_call(functools.partial(collect_body, offsets), out_shape=jax.Sh...  1.84 us
    pallas_call x1, Pallas kernels, products(): pl.pallas_call(own_product_body, out_shape=jax.ShapeDtypeStruct((2, group...  1.25 us
  transfers between devices with their start and end apart: 3, of which 3 were waited for; matrix products, arithmetic and copies ran while one was open for 0% of the time, Pallas kernels for 5%

profile of v3, /device:TPU:0, one launch (start us, length us, event | category | flops | bytes accessed | tf_op | source)
XLA Modules:
  0.0 60.9 jit_solution(10057478188583015991)
XLA Ops:
  0.0 10.4 %shard_map.91 = bf16[32,2,64,128]{3,2,1,0:T(8,128)(2,1)} custom-call(bf16[128,768]{1,0:T(8,128)(2,1)} %constant.10.clone.refs_0_, f32[64,256]{1,0:T(8,128)} %constant.11.clone.refs_1_, f32[64,256]{1,0:T(8,128)} %constant.12.clone.refs_2_, bf16[256,256]{1,0:T(8,128)(2,1)} %constant.13.clone.refs_3_, f32[64,128]{1,0:T(8,128)} %constant.14.clone.refs_4_, ...), custom_call_target="tpu_custom_call" | custom-call | flops 2147483648 | bytes 16777216 | tf_op jit(solution)/shard_map/pallas_call | solution.py:140
  10.4 33.7 %all_to_all.5.in_ref = bf16[32,2,64,128]{3,2,1,0:T(8,128)(2,1)S(1)} all-to-all(bf16[32,2,64,128]{3,2,1,0:T(8,128)(2,1)} %shard_map.91), channel_id=1, replica_groups=mesh['line'=1,'freq'=4,'section'=2,'rcv'=4] {'freq','section','rcv'}, dimensions={0} | all-to-all | bytes 2097152 | tf_op jit(solution)/shard_map/all_to_all | solution.py:304
  44.2 0.6 %shard_map.92 = (bf16[512,512]{1,0:T(8,128)(2,1)S(1)}, bf16[512,512]{1,0:T(8,128)(2,1)S(1)}, bf16[2,512,128]{2,1,0:T(8,128)(2,1)S(1)}) custom-call(bf16[32,2,64,128]{3,2,1,0:T(8,128)(2,1)S(1)} %all_to_all.5.in_ref), custom_call_target="tpu_custom_call" | custom-call | flops 268435456 | bytes 1048576 | tf_op jit(solution)/shard_map/pallas_call | solution.py:273
  44.8 2.3 %collective-permute-start.2 = (bf16[2,512,128]{2,1,0:T(8,128)(2,1)S(1)}, bf16[2,512,128]{2,1,0:T(8,128)(2,1)S(1)}, u32[]{:S(2)}, u32[]{:S(2)}) collective-permute-start(bf16[2,512,128]{2,1,0:T(8,128)(2,1)S(1)} %get-tuple-element.14), channel_id=1, source_target_pairs={{0,3},{1,2},{2,1},{3,0},{4,7},{5,6},{6,5},{7,4},{8,11},{9,10},{10,... | collective-permute-start | bytes 786440 | tf_op jit(solution)/shard_map/ppermute | solution.py:164
  47.1 0.7 %shard_map.93 = (bf16[2,512,128]{2,1,0:T(8,128)(2,1)S(1)}, bf16[2,512,128]{2,1,0:T(8,128)(2,1)S(1)}) custom-call(bf16[512,512]{1,0:T(8,128)(2,1)S(1)} %get-tuple-element.10.real_ref, bf16[512,512]{1,0:T(8,128)(2,1)S(1)} %get-tuple-element.11.imag_ref), custom_call_target="tpu_custom_call" | custom-call | flops 536870912 | bytes 1048576 | tf_op jit(solution)/shard_map/pallas_call | solution.py:280
  47.8 0.6 %collective-permute-start = (bf16[2,512,128]{2,1,0:T(8,128)(2,1)S(1)}, bf16[2,512,128]{2,1,0:T(8,128)(2,1)S(1)}, u32[]{:S(2)}, u32[]{:S(2)}) collective-permute-start(bf16[2,512,128]{2,1,0:T(8,128)(2,1)S(1)} %get-tuple-element.12), channel_id=1, source_target_pairs={{0,2},{1,3},{2,0},{3,1},{4,6},{5,7},{6,4},{7,5},{8,10},{9,11},{10,... | collective-permute-start | bytes 786440 | tf_op jit(solution)/shard_map/ppermute | solution.py:164
  48.4 0.7 %collective-permute-start.1 = (bf16[2,512,128]{2,1,0:T(8,128)(2,1)S(1)}, bf16[2,512,128]{2,1,0:T(8,128)(2,1)S(1)}, u32[]{:S(2)}, u32[]{:S(2)}) collective-permute-start(bf16[2,512,128]{2,1,0:T(8,128)(2,1)S(1)} %get-tuple-element.13), channel_id=1, source_target_pairs={{0,1},{1,0},{2,3},{3,2},{4,5},{5,4},{6,7},{7,6},{8,9},{9,8},{10,11... | collective-permute-start | bytes 786440 | tf_op jit(solution)/shard_map/ppermute | solution.py:164
  49.1 1.2 %shard_map.94.refs_1_ = f32[2,4,512,128]{3,2,1,0:T(8,128)} custom-call(bf16[512,512]{1,0:T(8,128)(2,1)S(1)} %get-tuple-element.10.real_ref, bf16[512,512]{1,0:T(8,128)(2,1)S(1)} %get-tuple-element.11.imag_ref), custom_call_target="tpu_custom_call" | custom-call | flops 268435456 | bytes 1048576 | tf_op jit(solution)/shard_map/pallas_call | solution.py:287
  50.4 4.6 %collective-permute-done.2.refs_0_ = bf16[2,512,128]{2,1,0:T(8,128)(2,1)S(1)} collective-permute-done((bf16[2,512,128]{2,1,0:T(8,128)(2,1)S(1)}, bf16[2,512,128]{2,1,0:T(8,128)(2,1)S(1)}, u32[]{:S(2)}, u32[]{:S(2)}) %collective-permute-start.2) | collective-permute-done | bytes 262176 | tf_op jit(solution)/shard_map/ppermute | solution.py:164
  55.0 0.8 %shard_map.95.refs_2_ = f32[2,4,512,128]{3,2,1,0:T(8,128)} custom-call(bf16[2,512,128]{2,1,0:T(8,128)(2,1)S(1)} %collective-permute-done.2.refs_0_, f32[2,4,512,128]{3,2,1,0:T(8,128)} %shard_map.94.refs_1_), custom_call_target="tpu_custom_call", output_to_operand_aliasing={{}: (1, {})} | custom-call | bytes 786432 | tf_op jit(solution)/shard_map/pallas_call | solution.py:242
  55.8 3.6 %collective-permute-done.refs_0_ = bf16[2,512,128]{2,1,0:T(8,128)(2,1)S(1)} collective-permute-done((bf16[2,512,128]{2,1,0:T(8,128)(2,1)S(1)}, bf16[2,512,128]{2,1,0:T(8,128)(2,1)S(1)}, u32[]{:S(2)}, u32[]{:S(2)}) %collective-permute-start) | collective-permute-done | bytes 262176 | tf_op jit(solution)/shard_map/ppermute | solution.py:164
  59.5 0.4 collective-permute-done.1.refs_1_
  59.9 1.0 %shard_map.96 = f32[2,4,512,128]{3,2,1,0:T(8,128)} custom-call(bf16[2,512,128]{2,1,0:T(8,128)(2,1)S(1)} %collective-permute-done.refs_0_, bf16[2,512,128]{2,1,0:T(8,128)(2,1)S(1)} %collective-permute-done.1.refs_1_, f32[2,4,512,128]{3,2,1,0:T(8,128)} %shard_map.95.refs_2_), custom_call_target="tpu_custom_call", output_to_operand_aliasing={{}: (2, {})} | custom-call | bytes 1572864 | tf_op jit(solution)/shard_map/pallas_call | solution.py:242
Async XLA Ops:
  44.8 10.2 %collective-permute-start.2 = (bf16[2,512,128]{2,1,0:T(8,128)(2,1)S(1)}, bf16[2,512,128]{2,1,0:T(8,128)(2,1)S(1)}, u32[]{:S(2)}, u32[]{:S(2)}) collective-permute-start(bf16[2,512,128]{2,1,0:T(8,128)(2,1)S(1)} %get-tuple-element.14), channel_id=1, source_target_pairs={{0,3},{1,2},{2,1},{3,0},{4,7},{5,6},{6,5},{7,4},{8,11},{9,10},{10,... | collective-permute-start | bytes 786440 | tf_op jit(solution)/shard_map/ppermute | solution.py:164
  47.8 11.7 %collective-permute-start = (bf16[2,512,128]{2,1,0:T(8,128)(2,1)S(1)}, bf16[2,512,128]{2,1,0:T(8,128)(2,1)S(1)}, u32[]{:S(2)}, u32[]{:S(2)}) collective-permute-start(bf16[2,512,128]{2,1,0:T(8,128)(2,1)S(1)} %get-tuple-element.12), channel_id=1, source_target_pairs={{0,2},{1,3},{2,0},{3,1},{4,6},{5,7},{6,4},{7,5},{8,10},{9,11},{10,... | collective-permute-start | bytes 786440 | tf_op jit(solution)/shard_map/ppermute | solution.py:164
  48.4 11.5 %collective-permute-start.1 = (bf16[2,512,128]{2,1,0:T(8,128)(2,1)S(1)}, bf16[2,512,128]{2,1,0:T(8,128)(2,1)S(1)}, u32[]{:S(2)}, u32[]{:S(2)}) collective-permute-start(bf16[2,512,128]{2,1,0:T(8,128)(2,1)S(1)} %get-tuple-element.13), channel_id=1, source_target_pairs={{0,1},{1,0},{2,3},{3,2},{4,5},{5,4},{6,7},{7,6},{8,9},{9,8},{10,11... | collective-permute-start | bytes 786440 | tf_op jit(solution)/shard_map/ppermute | solution.py:164

commit v4 on v3

--- a/solution.py
+++ b/solution.py
@@ -13,7 +13,7 @@
 REFLECTIVITY = 0.6
 LANES = 128
 BLOCK = 16
-ORDER = (3, 2, 1)
+STEPS = ((1, 2), (3, 3), (2, 1))
 SPECTRUM_VMEM = 56 * 2**20
 REGROUP_VMEM = 16 * 2**20
 PRODUCT_VMEM = 24 * 2**20
@@ -139,7 +139,7 @@
     operands = (*constants, signatures, ghost_delay, dead_trace, recorded)
     return pl.pallas_call(
         functools.partial(spectrum_body, bins, chunk),
-        in_specs=[pl.BlockSpec(memory_space=pl.ANY)] * len(operands),
+        in_specs=[pl.BlockSpec(memory_space=pltpu.HBM)] * len(operands),
         out_specs=pl.BlockSpec(memory_space=pltpu.VMEM),
         out_shape=jax.ShapeDtypeStruct((bins, 2, shots, receivers), jnp.bfloat16),
         scratch_shapes=[pltpu.VMEM(x.shape, x.dtype) for x in operands]
@@ -158,26 +158,33 @@
     return lax.axis_size("freq"), lax.axis_size("section"), lax.axis_size("rcv")
 
 
-def exchange(array, across):
-    if not across:
-        return array
-    return lax.ppermute(array, "rcv", [(c, c ^ across) for c in range(lax.axis_size("rcv"))])
+def exchange(array, step):
+    sections, groups = lax.axis_size("section"), lax.axis_size("rcv")
+    pairs = [
+        (s * groups + c, s * groups + (c ^ STEPS[step][s % 2]))
+        for s in range(sections)
+        for c in range(groups)
+    ]
+    return lax.ppermute(array, ("section", "rcv"), pairs)
+
+
+def partner(step):
+    even, odd = STEPS[step]
+    return lax.axis_index("rcv") ^ jnp.where(lax.axis_index("section") % 2 == 0, even, odd)
 
 
 def in_vmem(count):
     return [pl.BlockSpec(memory_space=pltpu.VMEM)] * count
 
 
-def own_columns(part_ref, across):
-    stations = part_ref.shape[0]
-    receivers = stations // lax.axis_size("rcv")
-    column = (lax.axis_index("rcv") ^ across) * receivers
-    return part_ref[:, pl.ds(pl.multiple_of(column, receivers), receivers)]
-
-
-def block_product(real_ref, imag_ref, across):
+def group_columns(part_ref, group):
+    receivers = part_ref.shape[0] // lax.axis_size("rcv")
+    return part_ref[:, pl.ds(pl.multiple_of(group * receivers, receivers), receivers)]
+
+
+def block_product(real_ref, imag_ref, group):
     stations = real_ref.shape[0]
-    real, imag = own_columns(real_ref, across), own_columns(imag_ref, across)
+    real, imag = group_columns(real_ref, group), group_columns(imag_ref, group)
     right = jnp.concatenate(
         [jnp.concatenate([real, imag], axis=1), jnp.concatenate([-imag, real], axis=1)]
     )
@@ -196,20 +203,20 @@
         columns = pl.ds(source % groups * receivers, receivers)
         real_ref[rows, columns] = in_ref[source, 0]
         imag_ref[rows, columns] = in_ref[source, 1]
-    for part, block in enumerate(block_product(real_ref, imag_ref, ORDER[0])):
+    for part, block in enumerate(block_product(real_ref, imag_ref, partner(0))):
         out_ref[part] = block.astype(out_ref.dtype)
 
 
 def other_product_body(real_ref, imag_ref, *out_refs):
-    for across, out_ref in zip(ORDER[1:], out_refs, strict=True):
-        for part, block in enumerate(block_product(real_ref, imag_ref, across)):
+    for step, out_ref in enumerate(out_refs, 1):
+        for part, block in enumerate(block_product(real_ref, imag_ref, partner(step))):
             out_ref[part] = block.astype(out_ref.dtype)
 
 
 def own_product_body(real_ref, imag_ref, result_ref, own_ref, sems):
     mine = lax.axis_index("rcv")
     copies = []
-    for part, block in enumerate(block_product(real_ref, imag_ref, 0)):
+    for part, block in enumerate(block_product(real_ref, imag_ref, mine)):
         own_ref[part] = block
         copy = pltpu.make_async_copy(
             own_ref.at[part], result_ref.at[part, mine], sems.at[part]
@@ -220,15 +227,14 @@
         copy.wait()
 
 
-def collect_body(offsets, *refs):
-    in_refs, (result_ref, wide_ref, sems) = refs[: len(offsets)], refs[-3:]
-    mine = lax.axis_index("rcv")
+def collect_body(steps, *refs):
+    in_refs, (result_ref, wide_ref, sems) = refs[: len(steps)], refs[-3:]
     copies = []
-    for i, (across, in_ref) in enumerate(zip(offsets, in_refs, strict=True)):
+    for i, (step, in_ref) in enumerate(zip(steps, in_refs, strict=True)):
         for part in range(2):
             wide_ref[i, part] = in_ref[part].astype(jnp.float32)
             copy = pltpu.make_async_copy(
-                wide_ref.at[i, part], result_ref.at[part, mine ^ across], sems.at[i, part]
+                wide_ref.at[i, part], result_ref.at[part, partner(step)], sems.at[i, part]
             )
             copy.start()
             copies.append(copy)
@@ -236,11 +242,11 @@
         copy.wait()
 
 
-def collect(arrays, offsets, result):
+def collect(arrays, steps, result):
     anywhere = pl.BlockSpec(memory_space=pl.ANY)
     count, size = len(arrays), arrays[0].size
     return pl.pallas_call(
-        functools.partial(collect_body, offsets),
+        functools.partial(collect_body, steps),
         out_shape=jax.ShapeDtypeStruct(result.shape, result.dtype),
         in_specs=in_vmem(count) + [anywhere],
         out_specs=anywhere,
@@ -303,9 +309,9 @@
     axes = ("freq", "section", "rcv")
     relayed = lax.all_to_all(deghosted, axes, split_axis=0, concat_axis=0, tiled=True)
     blocks, result = products(relayed)
-    arrived = [exchange(block, across) for across, block in zip(ORDER, blocks, strict=True)]
-    result = collect(arrived[:1], ORDER[:1], result)
-    return collect(arrived[1:], ORDER[1:], result)
+    arrived = [exchange(block, step) for step, block in enumerate(blocks)]
+    result = collect(arrived[:1], (0,), result)
+    return collect(arrived[1:], (1, 2), result)
 
 
 def solution(mesh):

time: 61.1 us -> 60.9 us (level)
  no operation moved by 1% of the time
where the time goes in v4:
time: 60.9 us; the launch traced here: 60.7 us
  blocking collectives  33.7 us (55%)
  Pallas kernels  14.9 us (24%)
  waiting for transfers between devices  8.48 us (14%)
  starting transfers between devices  3.62 us (6%)
    all_to_all x1, blocking collectives, per_device(): lax.all_to_all(deghosted, axes, split_axis=0, concat_axis=0, tiled=True)  33.7 us
    pallas_call x1, Pallas kernels, spectra(): pl.pallas_call(functools.partial(spectrum_body, bins, chunk), in_specs=[p...  10.4 us
    ppermute x3, waiting for transfers between devices, exchange(): return lax.ppermute(array, ('section', 'rcv'), pairs)  8.48 us
    ppermute x3, starting transfers between devices, exchange(): return lax.ppermute(array, ('section', 'rcv'), pairs)  3.62 us
    pallas_call x2, Pallas kernels, collect(): pl.pallas_call(functools.partial(collect_body, steps), out_shape=jax.Shap...  1.84 us
    pallas_call x1, Pallas kernels, products(): pl.pallas_call(own_product_body, out_shape=jax.ShapeDtypeStruct((2, group...  1.25 us
  transfers between devices with their start and end apart: 3, of which 3 were waited for; matrix products, arithmetic and copies ran while one was open for 0% of the time, Pallas kernels for 5%

profile of v4, /device:TPU:0, one launch (start us, length us, event | category | flops | bytes accessed | tf_op | source)
XLA Modules:
  0.0 60.7 jit_solution(5012398732952944553)
XLA Ops:
  0.0 10.4 %shard_map.91 = bf16[32,2,64,128]{3,2,1,0:T(8,128)(2,1)} custom-call(bf16[128,768]{1,0:T(8,128)(2,1)} %constant.10.clone.refs_0_, f32[64,256]{1,0:T(8,128)} %constant.11.clone.refs_1_, f32[64,256]{1,0:T(8,128)} %constant.12.clone.refs_2_, bf16[256,256]{1,0:T(8,128)(2,1)} %constant.13.clone.refs_3_, f32[64,128]{1,0:T(8,128)} %constant.14.clone.refs_4_, ...), custom_call_target="tpu_custom_call" | custom-call | flops 2147483648 | bytes 16777216 | tf_op jit(solution)/shard_map/pallas_call | solution.py:140
  10.4 33.7 %all_to_all.5.in_ref = bf16[32,2,64,128]{3,2,1,0:T(8,128)(2,1)S(1)} all-to-all(bf16[32,2,64,128]{3,2,1,0:T(8,128)(2,1)} %shard_map.91), channel_id=1, replica_groups=mesh['line'=1,'freq'=4,'section'=2,'rcv'=4] {'freq','section','rcv'}, dimensions={0} | all-to-all | bytes 2097152 | tf_op jit(solution)/shard_map/all_to_all | solution.py:310
  44.2 0.6 %shard_map.92 = (bf16[512,512]{1,0:T(8,128)(2,1)S(1)}, bf16[512,512]{1,0:T(8,128)(2,1)S(1)}, bf16[2,512,128]{2,1,0:T(8,128)(2,1)S(1)}) custom-call(bf16[32,2,64,128]{3,2,1,0:T(8,128)(2,1)S(1)} %all_to_all.5.in_ref), custom_call_target="tpu_custom_call" | custom-call | flops 268435456 | bytes 1048576 | tf_op jit(solution)/shard_map/pallas_call | solution.py:279
  44.8 1.4 %collective-permute-start.2 = (bf16[2,512,128]{2,1,0:T(8,128)(2,1)S(1)}, bf16[2,512,128]{2,1,0:T(8,128)(2,1)S(1)}, u32[]{:S(2)}, u32[]{:S(2)}) collective-permute-start(bf16[2,512,128]{2,1,0:T(8,128)(2,1)S(1)} %get-tuple-element.14), channel_id=1, source_target_pairs={{0,1},{1,0},{2,3},{3,2},{4,6},{5,7},{6,4},{7,5},{8,9},{9,8},{10,11... | collective-permute-start | bytes 786440 | tf_op jit(solution)/shard_map/ppermute | solution.py:168
  46.2 0.7 %shard_map.93 = (bf16[2,512,128]{2,1,0:T(8,128)(2,1)S(1)}, bf16[2,512,128]{2,1,0:T(8,128)(2,1)S(1)}) custom-call(bf16[512,512]{1,0:T(8,128)(2,1)S(1)} %get-tuple-element.10.real_ref, bf16[512,512]{1,0:T(8,128)(2,1)S(1)} %get-tuple-element.11.imag_ref), custom_call_target="tpu_custom_call" | custom-call | flops 536870912 | bytes 1048576 | tf_op jit(solution)/shard_map/pallas_call | solution.py:286
  46.9 1.5 %collective-permute-start = (bf16[2,512,128]{2,1,0:T(8,128)(2,1)S(1)}, bf16[2,512,128]{2,1,0:T(8,128)(2,1)S(1)}, u32[]{:S(2)}, u32[]{:S(2)}) collective-permute-start(bf16[2,512,128]{2,1,0:T(8,128)(2,1)S(1)} %get-tuple-element.12), channel_id=1, source_target_pairs={{0,3},{1,2},{2,1},{3,0},{4,7},{5,6},{6,5},{7,4},{8,11},{9,10},{10,... | collective-permute-start | bytes 786440 | tf_op jit(solution)/shard_map/ppermute | solution.py:168
  48.4 0.7 %collective-permute-start.1 = (bf16[2,512,128]{2,1,0:T(8,128)(2,1)S(1)}, bf16[2,512,128]{2,1,0:T(8,128)(2,1)S(1)}, u32[]{:S(2)}, u32[]{:S(2)}) collective-permute-start(bf16[2,512,128]{2,1,0:T(8,128)(2,1)S(1)} %get-tuple-element.13), channel_id=1, source_target_pairs={{0,2},{1,3},{2,0},{3,1},{4,5},{5,4},{6,7},{7,6},{8,10},{9,11},{10,... | collective-permute-start | bytes 786440 | tf_op jit(solution)/shard_map/ppermute | solution.py:168
  49.2 1.3 %shard_map.94.refs_1_ = f32[2,4,512,128]{3,2,1,0:T(8,128)} custom-call(bf16[512,512]{1,0:T(8,128)(2,1)S(1)} %get-tuple-element.10.real_ref, bf16[512,512]{1,0:T(8,128)(2,1)S(1)} %get-tuple-element.11.imag_ref), custom_call_target="tpu_custom_call" | custom-call | flops 268435456 | bytes 1048576 | tf_op jit(solution)/shard_map/pallas_call | solution.py:293
  50.4 2.7 %collective-permute-done.2.refs_0_ = bf16[2,512,128]{2,1,0:T(8,128)(2,1)S(1)} collective-permute-done((bf16[2,512,128]{2,1,0:T(8,128)(2,1)S(1)}, bf16[2,512,128]{2,1,0:T(8,128)(2,1)S(1)}, u32[]{:S(2)}, u32[]{:S(2)}) %collective-permute-start.2) | collective-permute-done | bytes 262176 | tf_op jit(solution)/shard_map/ppermute | solution.py:168
  53.1 0.8 %shard_map.95.refs_2_ = f32[2,4,512,128]{3,2,1,0:T(8,128)} custom-call(bf16[2,512,128]{2,1,0:T(8,128)(2,1)S(1)} %collective-permute-done.2.refs_0_, f32[2,4,512,128]{3,2,1,0:T(8,128)} %shard_map.94.refs_1_), custom_call_target="tpu_custom_call", output_to_operand_aliasing={{}: (1, {})} | custom-call | bytes 786432 | tf_op jit(solution)/shard_map/pallas_call | solution.py:248
  53.9 5.0 %collective-permute-done.refs_0_ = bf16[2,512,128]{2,1,0:T(8,128)(2,1)S(1)} collective-permute-done((bf16[2,512,128]{2,1,0:T(8,128)(2,1)S(1)}, bf16[2,512,128]{2,1,0:T(8,128)(2,1)S(1)}, u32[]{:S(2)}, u32[]{:S(2)}) %collective-permute-start) | collective-permute-done | bytes 262176 | tf_op jit(solution)/shard_map/ppermute | solution.py:168
  59.0 0.8 %collective-permute-done.1.refs_1_ = bf16[2,512,128]{2,1,0:T(8,128)(2,1)S(1)} collective-permute-done((bf16[2,512,128]{2,1,0:T(8,128)(2,1)S(1)}, bf16[2,512,128]{2,1,0:T(8,128)(2,1)S(1)}, u32[]{:S(2)}, u32[]{:S(2)}) %collective-permute-start.1) | collective-permute-done | bytes 262176 | tf_op jit(solution)/shard_map/ppermute | solution.py:168
  59.7 1.0 %shard_map.96 = f32[2,4,512,128]{3,2,1,0:T(8,128)} custom-call(bf16[2,512,128]{2,1,0:T(8,128)(2,1)S(1)} %collective-permute-done.refs_0_, bf16[2,512,128]{2,1,0:T(8,128)(2,1)S(1)} %collective-permute-done.1.refs_1_, f32[2,4,512,128]{3,2,1,0:T(8,128)} %shard_map.95.refs_2_), custom_call_target="tpu_custom_call", output_to_operand_aliasing={{}: (2, {})} | custom-call | bytes 1572864 | tf_op jit(solution)/shard_map/pallas_call | solution.py:248
Async XLA Ops:
  44.8 8.3 %collective-permute-start.2 = (bf16[2,512,128]{2,1,0:T(8,128)(2,1)S(1)}, bf16[2,512,128]{2,1,0:T(8,128)(2,1)S(1)}, u32[]{:S(2)}, u32[]{:S(2)}) collective-permute-start(bf16[2,512,128]{2,1,0:T(8,128)(2,1)S(1)} %get-tuple-element.14), channel_id=1, source_target_pairs={{0,1},{1,0},{2,3},{3,2},{4,6},{5,7},{6,4},{7,5},{8,9},{9,8},{10,11... | collective-permute-start | bytes 786440 | tf_op jit(solution)/shard_map/ppermute | solution.py:168
  46.9 12.0 %collective-permute-start = (bf16[2,512,128]{2,1,0:T(8,128)(2,1)S(1)}, bf16[2,512,128]{2,1,0:T(8,128)(2,1)S(1)}, u32[]{:S(2)}, u32[]{:S(2)}) collective-permute-start(bf16[2,512,128]{2,1,0:T(8,128)(2,1)S(1)} %get-tuple-element.12), channel_id=1, source_target_pairs={{0,3},{1,2},{2,1},{3,0},{4,7},{5,6},{6,5},{7,4},{8,11},{9,10},{10,... | collective-permute-start | bytes 786440 | tf_op jit(solution)/shard_map/ppermute | solution.py:168
  48.4 11.3 %collective-permute-start.1 = (bf16[2,512,128]{2,1,0:T(8,128)(2,1)S(1)}, bf16[2,512,128]{2,1,0:T(8,128)(2,1)S(1)}, u32[]{:S(2)}, u32[]{:S(2)}) collective-permute-start(bf16[2,512,128]{2,1,0:T(8,128)(2,1)S(1)} %get-tuple-element.13), channel_id=1, source_target_pairs={{0,2},{1,3},{2,0},{3,1},{4,5},{5,4},{6,7},{7,6},{8,10},{9,11},{10,... | collective-permute-start | bytes 786440 | tf_op jit(solution)/shard_map/ppermute | solution.py:168

commit v5 on v4

--- a/solution.py
+++ b/solution.py
@@ -310,8 +310,9 @@
     relayed = lax.all_to_all(deghosted, axes, split_axis=0, concat_axis=0, tiled=True)
     blocks, result = products(relayed)
     arrived = [exchange(block, step) for step, block in enumerate(blocks)]
-    result = collect(arrived[:1], (0,), result)
-    return collect(arrived[1:], (1, 2), result)
+    for step, block in enumerate(arrived):
+        result = collect([block], (step,), result)
+    return result
 
 
 def solution(mesh):

time: 60.9 us -> 60.8 us (level)
  waiting for transfers between devices: 8.48 us -> 7.7 us
    ppermute x3, waiting for transfers between devices: 8.48 us -> 7.7 us  [exchange(): return lax.ppermute(array, ('section', 'rcv'), pairs)]
    pallas_call x2 -> x3, Pallas kernels: 1.84 us -> 2.47 us  [collect(): pl.pallas_call(functools.partial(collect_body, steps), out_shape=jax.Shap...]
  transfers between devices with their start and end apart: 3 -> 3, of which waited for: 3 -> 2; matrix products, arithmetic and copies ran while one was open for 0% -> 0% of each run, Pallas kernels for 5% -> 6%
where the time goes in v5:
time: 60.8 us; the launch traced here: 60.6 us
  blocking collectives  33.7 us (55%)
  Pallas kernels  15.5 us (25%)
  waiting for transfers between devices  7.7 us (13%)
  starting transfers between devices  3.62 us (6%)
    all_to_all x1, blocking collectives, per_device(): lax.all_to_all(deghosted, axes, split_axis=0, concat_axis=0, tiled=True)  33.7 us
    pallas_call x1, Pallas kernels, spectra(): pl.pallas_call(functools.partial(spectrum_body, bins, chunk), in_specs=[p...  10.4 us
    ppermute x3, waiting for transfers between devices, exchange(): return lax.ppermute(array, ('section', 'rcv'), pairs)  7.7 us
    ppermute x3, starting transfers between devices, exchange(): return lax.ppermute(array, ('section', 'rcv'), pairs)  3.62 us
    pallas_call x3, Pallas kernels, collect(): pl.pallas_call(functools.partial(collect_body, steps), out_shape=jax.Shap...  2.47 us
    pallas_call x1, Pallas kernels, products(): pl.pallas_call(own_product_body, out_shape=jax.ShapeDtypeStruct((2, group...  1.25 us
  transfers between devices with their start and end apart: 3, of which 2 were waited for; matrix products, arithmetic and copies ran while one was open for 0% of the time, Pallas kernels for 6%

profile of v5, /device:TPU:0, one launch (start us, length us, event | category | flops | bytes accessed | tf_op | source)
XLA Modules:
  0.0 60.6 jit_solution(5444276124710041690)
XLA Ops:
  0.0 10.4 %shard_map.91 = bf16[32,2,64,128]{3,2,1,0:T(8,128)(2,1)} custom-call(bf16[128,768]{1,0:T(8,128)(2,1)} %constant.10.clone.refs_0_, f32[64,256]{1,0:T(8,128)} %constant.11.clone.refs_1_, f32[64,256]{1,0:T(8,128)} %constant.12.clone.refs_2_, bf16[256,256]{1,0:T(8,128)(2,1)} %constant.13.clone.refs_3_, f32[64,128]{1,0:T(8,128)} %constant.14.clone.refs_4_, ...), custom_call_target="tpu_custom_call" | custom-call | flops 2147483648 | bytes 16777216 | tf_op jit(solution)/shard_map/pallas_call | solution.py:140
  10.4 33.7 %all_to_all.5.in_ref = bf16[32,2,64,128]{3,2,1,0:T(8,128)(2,1)S(1)} all-to-all(bf16[32,2,64,128]{3,2,1,0:T(8,128)(2,1)} %shard_map.91), channel_id=1, replica_groups=mesh['line'=1,'freq'=4,'section'=2,'rcv'=4] {'freq','section','rcv'}, dimensions={0} | all-to-all | bytes 2097152 | tf_op jit(solution)/shard_map/all_to_all | solution.py:310
  44.2 0.6 %shard_map.92 = (bf16[512,512]{1,0:T(8,128)(2,1)S(1)}, bf16[512,512]{1,0:T(8,128)(2,1)S(1)}, bf16[2,512,128]{2,1,0:T(8,128)(2,1)S(1)}) custom-call(bf16[32,2,64,128]{3,2,1,0:T(8,128)(2,1)S(1)} %all_to_all.5.in_ref), custom_call_target="tpu_custom_call" | custom-call | flops 268435456 | bytes 1048576 | tf_op jit(solution)/shard_map/pallas_call | solution.py:279
  44.8 1.4 %collective-permute-start.2 = (bf16[2,512,128]{2,1,0:T(8,128)(2,1)S(1)}, bf16[2,512,128]{2,1,0:T(8,128)(2,1)S(1)}, u32[]{:S(2)}, u32[]{:S(2)}) collective-permute-start(bf16[2,512,128]{2,1,0:T(8,128)(2,1)S(1)} %get-tuple-element.14), channel_id=1, source_target_pairs={{0,1},{1,0},{2,3},{3,2},{4,6},{5,7},{6,4},{7,5},{8,9},{9,8},{10,11... | collective-permute-start | bytes 786440 | tf_op jit(solution)/shard_map/ppermute | solution.py:168
  46.2 0.7 %shard_map.93 = (bf16[2,512,128]{2,1,0:T(8,128)(2,1)S(1)}, bf16[2,512,128]{2,1,0:T(8,128)(2,1)S(1)}) custom-call(bf16[512,512]{1,0:T(8,128)(2,1)S(1)} %get-tuple-element.10.real_ref, bf16[512,512]{1,0:T(8,128)(2,1)S(1)} %get-tuple-element.11.imag_ref), custom_call_target="tpu_custom_call" | custom-call | flops 536870912 | bytes 1048576 | tf_op jit(solution)/shard_map/pallas_call | solution.py:286
  46.9 1.5 %collective-permute-start.1 = (bf16[2,512,128]{2,1,0:T(8,128)(2,1)S(1)}, bf16[2,512,128]{2,1,0:T(8,128)(2,1)S(1)}, u32[]{:S(2)}, u32[]{:S(2)}) collective-permute-start(bf16[2,512,128]{2,1,0:T(8,128)(2,1)S(1)} %get-tuple-element.13), channel_id=1, source_target_pairs={{0,3},{1,2},{2,1},{3,0},{4,7},{5,6},{6,5},{7,4},{8,11},{9,10},{10,... | collective-permute-start | bytes 786440 | tf_op jit(solution)/shard_map/ppermute | solution.py:168
  48.4 0.7 %collective-permute-start = (bf16[2,512,128]{2,1,0:T(8,128)(2,1)S(1)}, bf16[2,512,128]{2,1,0:T(8,128)(2,1)S(1)}, u32[]{:S(2)}, u32[]{:S(2)}) collective-permute-start(bf16[2,512,128]{2,1,0:T(8,128)(2,1)S(1)} %get-tuple-element.12), channel_id=1, source_target_pairs={{0,2},{1,3},{2,0},{3,1},{4,5},{5,4},{6,7},{7,6},{8,10},{9,11},{10,... | collective-permute-start | bytes 786440 | tf_op jit(solution)/shard_map/ppermute | solution.py:168
  49.2 1.3 %shard_map.94.refs_1_ = f32[2,4,512,128]{3,2,1,0:T(8,128)} custom-call(bf16[512,512]{1,0:T(8,128)(2,1)S(1)} %get-tuple-element.10.real_ref, bf16[512,512]{1,0:T(8,128)(2,1)S(1)} %get-tuple-element.11.imag_ref), custom_call_target="tpu_custom_call" | custom-call | flops 268435456 | bytes 1048576 | tf_op jit(solution)/shard_map/pallas_call | solution.py:293
  50.4 2.7 %collective-permute-done.2.refs_0_ = bf16[2,512,128]{2,1,0:T(8,128)(2,1)S(1)} collective-permute-done((bf16[2,512,128]{2,1,0:T(8,128)(2,1)S(1)}, bf16[2,512,128]{2,1,0:T(8,128)(2,1)S(1)}, u32[]{:S(2)}, u32[]{:S(2)}) %collective-permute-start.2) | collective-permute-done | bytes 262176 | tf_op jit(solution)/shard_map/ppermute | solution.py:168
  53.1 0.8 %shard_map.95.refs_1_ = f32[2,4,512,128]{3,2,1,0:T(8,128)} custom-call(bf16[2,512,128]{2,1,0:T(8,128)(2,1)S(1)} %collective-permute-done.2.refs_0_, f32[2,4,512,128]{3,2,1,0:T(8,128)} %shard_map.94.refs_1_), custom_call_target="tpu_custom_call", output_to_operand_aliasing={{}: (1, {})} | custom-call | bytes 786432 | tf_op jit(solution)/shard_map/pallas_call | solution.py:248
  53.9 5.0 %collective-permute-done.1.refs_0_ = bf16[2,512,128]{2,1,0:T(8,128)(2,1)S(1)} collective-permute-done((bf16[2,512,128]{2,1,0:T(8,128)(2,1)S(1)}, bf16[2,512,128]{2,1,0:T(8,128)(2,1)S(1)}, u32[]{:S(2)}, u32[]{:S(2)}) %collective-permute-start.1) | collective-permute-done | bytes 262176 | tf_op jit(solution)/shard_map/ppermute | solution.py:168
  59.0 0.8 %shard_map.96.refs_1_ = f32[2,4,512,128]{3,2,1,0:T(8,128)} custom-call(bf16[2,512,128]{2,1,0:T(8,128)(2,1)S(1)} %collective-permute-done.1.refs_0_, f32[2,4,512,128]{3,2,1,0:T(8,128)} %shard_map.95.refs_1_), custom_call_target="tpu_custom_call", output_to_operand_aliasing={{}: (1, {})} | custom-call | bytes 786432 | tf_op jit(solution)/shard_map/pallas_call | solution.py:248
  59.8 0.0 collective-permute-done.refs_0_
  59.8 0.8 %shard_map.97 = f32[2,4,512,128]{3,2,1,0:T(8,128)} custom-call(bf16[2,512,128]{2,1,0:T(8,128)(2,1)S(1)} %collective-permute-done.refs_0_, f32[2,4,512,128]{3,2,1,0:T(8,128)} %shard_map.96.refs_1_), custom_call_target="tpu_custom_call", output_to_operand_aliasing={{}: (1, {})} | custom-call | bytes 786432 | tf_op jit(solution)/shard_map/pallas_call | solution.py:248
Async XLA Ops:
  44.8 8.3 %collective-permute-start.2 = (bf16[2,512,128]{2,1,0:T(8,128)(2,1)S(1)}, bf16[2,512,128]{2,1,0:T(8,128)(2,1)S(1)}, u32[]{:S(2)}, u32[]{:S(2)}) collective-permute-start(bf16[2,512,128]{2,1,0:T(8,128)(2,1)S(1)} %get-tuple-element.14), channel_id=1, source_target_pairs={{0,1},{1,0},{2,3},{3,2},{4,6},{5,7},{6,4},{7,5},{8,9},{9,8},{10,11... | collective-permute-start | bytes 786440 | tf_op jit(solution)/shard_map/ppermute | solution.py:168
  46.9 12.0 %collective-permute-start.1 = (bf16[2,512,128]{2,1,0:T(8,128)(2,1)S(1)}, bf16[2,512,128]{2,1,0:T(8,128)(2,1)S(1)}, u32[]{:S(2)}, u32[]{:S(2)}) collective-permute-start(bf16[2,512,128]{2,1,0:T(8,128)(2,1)S(1)} %get-tuple-element.13), channel_id=1, source_target_pairs={{0,3},{1,2},{2,1},{3,0},{4,7},{5,6},{6,5},{7,4},{8,11},{9,10},{10,... | collective-permute-start | bytes 786440 | tf_op jit(solution)/shard_map/ppermute | solution.py:168
  48.4 11.4 %collective-permute-start = (bf16[2,512,128]{2,1,0:T(8,128)(2,1)S(1)}, bf16[2,512,128]{2,1,0:T(8,128)(2,1)S(1)}, u32[]{:S(2)}, u32[]{:S(2)}) collective-permute-start(bf16[2,512,128]{2,1,0:T(8,128)(2,1)S(1)} %get-tuple-element.12), channel_id=1, source_target_pairs={{0,2},{1,3},{2,0},{3,1},{4,5},{5,4},{6,7},{7,6},{8,10},{9,11},{10,... | collective-permute-start | bytes 786440 | tf_op jit(solution)/shard_map/ppermute | solution.py:168
